TPU v7x, 256 devices: a whole 4x4x8 slice. The times are simulated.
256 devices in a mesh: det: 32 (over x, z), tile: 8 (over y, core).
Axes of the slice: x: 4, y: 4, z: 8, core: 2. Of those that a mesh axis runs over, the one named last changes fastest.
Arguments:
- detector_samples: float32 [128, 32768], P('det', 'tile'), may hold values from -180 to 180
- pixels: int32 [128, 32768], P('det', 'tile'), may hold values from 0 to 16383
- crossings: int32 [128, 8, 4], P('det', 'tile'), may hold values from 0 to 511, as said below
- lengths: int32 [128, 8, 16], P('det', 'tile'), may hold values from 1 to 512, 4096 in all within a row
- mode_templates: float32 [128, 64], replicated, may hold values from -0.5 to 0.5
- mixing: float32 [64, 64], replicated, may hold values from -0.2 to 1
- sky_map: float32 [512, 128, 128], P(('det', 'tile')), may hold values from -6 to 6
Outputs:
- sky_estimate: float32 [512, 128, 128], P(('det', 'tile'))
- baseline_fit: float32 [128, 8, 16], P('det', 'tile')
Inputs may be any that keep to these rules, and one draw needn't show every extreme that they name: `crossings`: tile g is owned by device g // 2 of det+tile. In each time block, the entries of the 4 detectors of one det index name exactly 16 distinct tiles, owned by 16 different devices whose tile index is the block's, each tile named by exactly 1 of these entries.
All inputs are finite; a program needn't handle non-finite values.
Results may differ from a plain program's by a relative error of at most 0.0015.
Values may be sent and summed in bfloat16 or wider, within the bound.
A program may use at most 64 MiB of HBM per device.

v0:
```python
import jax
import jax.numpy as jnp
from jax import lax
from jax.sharding import PartitionSpec as P

SIDE = 128
PIX = 16384
TILE_DEV = 2
DETECTORS_LOCAL = 4
SAMP_DEV = 4096
SEG_PER = 4
BASELINE_COUNT = 16
ITERS = 2


HUBER = 1.345
EPS = 1e-05


def project(tile_table, table_slot, pixel_rows, pixel_cols, indices, per_turn):
    turn_count = table_slot.shape[0] // per_turn

    def project_group(inputs):
        slot_group, row_group, col_group = inputs
        chosen_entries = jnp.take(tile_table, slot_group, axis=0)
        row_onehot = (row_group[:, :, None] == indices).astype(jnp.bfloat16)
        selected_entries = jnp.einsum(
            "aqe,aeo->aqo", row_onehot, chosen_entries, preferred_element_type=jnp.float32
        )
        return jnp.sum(jnp.where(col_group[:, :, None] == indices, selected_entries, 0.0), axis=2)

    return lax.map(
        project_group,
        (
            table_slot.reshape(turn_count, per_turn),
            pixel_rows.reshape(turn_count, per_turn, -1),
            pixel_cols.reshape(turn_count, per_turn, -1),
        ),
    )


def local(detector_samples, pixels, crossings, lengths, mode_templates, mixing, sky_map):
    groups = lax.axis_size("det")
    blocks = lax.axis_size("tile")
    entries = DETECTORS_LOCAL * SEG_PER
    part_length = SAMP_DEV // SEG_PER
    tile_ids = crossings.reshape(entries)
    owner_flat = tile_ids // TILE_DEV
    owner_det = owner_flat // blocks
    local_tile = tile_ids % TILE_DEV
    indices = jnp.arange(SIDE, dtype=jnp.int32)
    pixel_parts = pixels.reshape(entries, part_length)
    pixel_rows = pixel_parts // SIDE
    pixel_cols = pixel_parts % SIDE
    per_turn = 4
    segment_ends = jnp.cumsum(lengths.reshape(DETECTORS_LOCAL, BASELINE_COUNT), axis=1)
    position = jnp.arange(SAMP_DEV, dtype=jnp.int32)
    segment_index = jnp.sum(
        (position[None, None, :] >= segment_ends[:, :, None]).astype(jnp.int32), axis=1
    )
    member_flags = (
        segment_index[:, None, :] == jnp.arange(BASELINE_COUNT, dtype=jnp.int32)[None, :, None]
    )
    table_rows = groups * TILE_DEV
    table_slot = owner_det * TILE_DEV + local_tile
    table_slot = owner_det
    matches = owner_det[None, :] == jnp.arange(groups, dtype=jnp.int32)[:, None]
    wanted = jnp.max(jnp.where(matches, local_tile[None, :], -1), axis=1)
    requested = lax.all_to_all(
        wanted.reshape(groups, 1), "det", split_axis=0, concat_axis=0, tiled=True
    ).reshape(groups)
    table_rows = groups
    flat_index = (table_slot[:, None] * PIX + pixel_parts).reshape(-1)
    current_estimate = sky_map
    baseline_values = jnp.zeros((DETECTORS_LOCAL, BASELINE_COUNT), jnp.float32)
    for iteration in range(ITERS):
        owned_tiles = current_estimate.astype(jnp.bfloat16)
        picked = jnp.take(owned_tiles, jnp.maximum(requested, 0), axis=0)
        outgoing = jnp.where((requested >= 0)[:, None, None], picked, jnp.zeros_like(picked))
        tile_table = lax.all_to_all(outgoing, "det", split_axis=0, concat_axis=0, tiled=True)
        pointed_pixels = project(
            tile_table, table_slot, pixel_rows, pixel_cols, indices, per_turn
        ).reshape(DETECTORS_LOCAL, SAMP_DEV)
        offset_values = jnp.sum(jnp.where(member_flags, baseline_values[:, :, None], 0.0), axis=1)
        residual_signal = detector_samples - pointed_pixels - offset_values
        my_templates = lax.dynamic_slice_in_dim(
            mode_templates, lax.axis_index("det") * DETECTORS_LOCAL, DETECTORS_LOCAL, 0
        )
        projected = lax.psum(
            jnp.dot(my_templates.T, residual_signal, precision=lax.Precision.HIGHEST), "det"
        )
        amplitudes = jnp.dot(mixing, projected, precision=lax.Precision.HIGHEST)
        cleaned = residual_signal - jnp.dot(
            my_templates, amplitudes, precision=lax.Precision.HIGHEST
        )
        squares = lax.psum(jnp.sum(cleaned * cleaned, axis=1), "tile")
        noise_level = jnp.sqrt(squares / (SAMP_DEV * blocks) + EPS)[:, None]
        weight = HUBER * noise_level / jnp.maximum(jnp.abs(cleaned), HUBER * noise_level)
        numerator = jnp.sum(jnp.where(member_flags, (weight * cleaned)[:, None, :], 0.0), axis=2)
        denominator = jnp.sum(jnp.where(member_flags, weight[:, None, :], 0.0), axis=2)
        baseline_step = numerator / denominator
        baseline_values = baseline_values + baseline_step
        remainder = cleaned - jnp.sum(
            jnp.where(member_flags, baseline_step[:, :, None], 0.0), axis=1
        )
        value_sums = (
            jnp.zeros((table_rows * PIX,), jnp.float32)
            .at[flat_index]
            .add((weight * remainder).reshape(-1))
        )
        weight_sums = (
            jnp.zeros((table_rows * PIX,), jnp.float32).at[flat_index].add(weight.reshape(-1))
        )
        stacked = jnp.stack(
            [value_sums.reshape(table_rows, PIX), weight_sums.reshape(table_rows, PIX)], axis=1
        )
        arrived = lax.all_to_all(stacked, "det", split_axis=0, concat_axis=0, tiled=True)
        chooser = (requested[None, :] == jnp.arange(TILE_DEV, dtype=jnp.int32)[:, None]).astype(
            jnp.float32
        )
        gathered = jnp.dot(
            chooser, arrived.reshape(groups, 2 * PIX), precision=lax.Precision.HIGHEST
        ).reshape(TILE_DEV, 2, PIX)
        current_estimate = current_estimate + (
            gathered[:, 0, :] / jnp.maximum(gathered[:, 1, :], 1.0)
        ).reshape(TILE_DEV, SIDE, SIDE)
    return (current_estimate, baseline_values.reshape(DETECTORS_LOCAL, 1, BASELINE_COUNT))


def solution(mesh):
    placed = (
        P("det", "tile"),
        P("det", "tile"),
        P("det", "tile", None),
        P("det", "tile", None),
        P(),
        P(),
        P(("det", "tile"), None, None),
    )
    return jax.shard_map(
        local,
        mesh=mesh,
        in_specs=placed,
        out_specs=(P(("det", "tile"), None, None), P("det", "tile", None)),
        check_vma=False,
    )
```

profile of v0, /device:TPU:1, one launch (start us, length us, event | category | flops | bytes accessed | tf_op | source)
XLA Modules:
  0.0 1014.2 jit_solution(12422058183509991935)
XLA Ops:
  7.7 1.3 reduce.6
  9.2 0.7 copy.41
  9.9 11.9 %all-to-all-start = ((s32[32,1,1]{2,1,0:T(1,128)}), s32[32,1,1]{2,1,0:T(1,128)S(1)}, u32[]{:S(2)}, u32[]{:S(2)}) async-start(s32[32,1,1]{2,1,0:T(1,128)} %copy.41), calls=%async_computation | async-start | bytes 32768 | tf_op jit(solution)/shard_map/all_to_all | solution.py:69
  21.8 0.9 convert_element_type.8
  22.7 7.6 all-to-all-done
  30.4 0.7 reduce.1
  31.1 0.7 gather_fusion.2
  31.8 0.7 compare_reduce_fusion
  32.5 1.2 select_select_fusion.1
  33.7 3.9 all-to-all-start.1
  38.1 23.9 %all-to-all-done.1 = bf16[32,128,128]{2,1,0:T(8,128)(2,1)S(1)} async-done(((bf16[32,128,128]{2,1,0:T(8,128)(2,1)}), bf16[32,128,128]{2,1,0:T(8,128)(2,1)S(1)}, u32[]{:S(2)}, u32[]{:S(2)}) %all-to-all-start.1) | async-done | bytes 1048608 | tf_op jit(solution)/shard_map/all_to_all | solution.py:80
  62.1 5.9 while.24
  62.1 0.6 gather_fusion
  62.7 0.8 select_reduce_fusion.11
  63.6 0.6 gather_fusion
  64.2 0.8 select_reduce_fusion.11
  65.7 0.8 select_reduce_fusion.11
  67.1 0.8 select_reduce_fusion.11
  68.1 2.1 fusion.42
  70.8 145.6 %all-reduce.3.cloned.1.call-done = f32[64,4096]{1,0:T(8,128)} async-done(((f32[64,4096]{1,0:T(8,128)}), f32[64,4096]{1,0:T(8,128)}) %all-reduce.3.cloned.1.call-update) | async-done | bytes 1048592 | tf_op jit(solution)/shard_map/psum | solution.py:89
  216.4 2.3 fusion.59
  218.7 0.8 multiply_reduce_fusion.1
  219.5 17.0 %psum.29 = f32[4]{0:T(128)S(1)} all-reduce(f32[4]{0:T(128)S(1)} %get-tuple-element.207), channel_id=1, replica_groups=mesh['det'=32,'tile'=8] {'tile'}, use_global_device_ids=true, to_apply=%region_6.9 | all-reduce | flops 4 | bytes 32 | tf_op jit(solution)/shard_map/psum | solution.py:96
  237.4 86.3 %scatter_custom_fusion = f32[524288]{0:T(1024)S(1)} fusion(s32[16384]{0:T(1024)S(1)} %bitcast.130, f32[16384]{0:T(1024)S(1)} %bitcast.135, f32[]{:T(128)} %constant.133.clone.1), kind=kCustom, calls=%fused_computation.71 | custom fusion | flops 16384 | bytes 2097156 | tf_op jit(solution)/shard_map/scatter-add | solution.py:109
  323.7 87.7 %scatter_custom_fusion.1 = f32[524288]{0:T(1024)} fusion(s32[16384]{0:T(1024)S(1)} %bitcast.131, f32[16384]{0:T(1024)S(1)} %bitcast.136, f32[]{:T(128)} %constant.133.clone.1), kind=kCustom, calls=%fused_computation.69 | custom fusion | flops 16384 | bytes 2097156 | tf_op jit(solution)/shard_map/scatter-add | solution.py:112
  411.4 5.6 pad_maximum_fusion
  417.1 97.4 %all_to_all.29 = f32[32,2,16384]{2,1,0:T(2,128)S(1)} all-to-all(f32[32,2,16384]{2,1,0:T(2,128)S(1)} %pad_maximum_fusion), channel_id=1, replica_groups=mesh['det'=32,'tile'=8] {'det'}, dimensions={0} | all-to-all | bytes 8388608 | tf_op jit(solution)/shard_map/all_to_all | solution.py:117
  514.5 3.8 fusion.21
  518.4 0.7 gather_fusion.3
  519.4 33.4 %all_to_all.30 = bf16[32,128,128]{2,1,0:T(8,128)(2,1)S(1)} all-to-all(bf16[32,128,128]{2,1,0:T(8,128)(2,1)S(1)} %select_select_fusion), channel_id=1, replica_groups=mesh['det'=32,'tile'=8] {'det'}, dimensions={0} | all-to-all | bytes 2097152 | tf_op jit(solution)/shard_map/all_to_all | solution.py:80
  552.8 5.9 while.25
  553.4 0.8 select_reduce_fusion.12
  554.3 0.6 gather_fusion.1
  554.9 0.8 select_reduce_fusion.12
  556.4 0.8 select_reduce_fusion.12
  557.9 0.8 select_reduce_fusion.12
  558.8 2.1 fusion.39
  560.9 143.3 %all-reduce.5.cloned.1.call-done = f32[64,4096]{1,0:T(8,128)} async-done(((f32[64,4096]{1,0:T(8,128)}), f32[64,4096]{1,0:T(8,128)}) %all-reduce.5.cloned.1.call-update) | async-done | bytes 1048592 | tf_op jit(solution)/shard_map/psum | solution.py:89
  704.1 2.3 fusion.60
  706.4 0.8 multiply_reduce_fusion
  707.2 17.0 %psum.31 = f32[4]{0:T(128)S(1)} all-reduce(f32[4]{0:T(128)S(1)} %get-tuple-element.209), channel_id=1, replica_groups=mesh['det'=32,'tile'=8] {'tile'}, use_global_device_ids=true, to_apply=%region_19.22 | all-reduce | flops 4 | bytes 32 | tf_op jit(solution)/shard_map/psum | solution.py:96
  724.7 0.6 fusion.56
  725.7 86.3 %scatter_custom_fusion.2 = f32[524288]{0:T(1024)S(1)} fusion(s32[16384]{0:T(1024)S(1)} %bitcast.132, f32[16384]{0:T(1024)S(1)} %bitcast.137, f32[]{:T(128)} %constant.133.clone.1), kind=kCustom, calls=%fused_computation.67 | custom fusion | flops 16384 | bytes 2097156 | tf_op jit(solution)/shard_map/scatter-add | solution.py:109
  812.0 87.3 %scatter_custom_fusion.3 = f32[524288]{0:T(1024)} fusion(s32[16384]{0:T(1024)S(1)} %bitcast.133, f32[16384]{0:T(1024)S(1)} %bitcast.134, f32[]{:T(128)} %constant.133.clone.1), kind=kCustom, calls=%fused_computation.65 | custom fusion | flops 16384 | bytes 2097156 | tf_op jit(solution)/shard_map/scatter-add | solution.py:112
  899.3 5.6 pad_maximum_fusion.1
  904.9 97.6 %all_to_all.31 = f32[32,2,16384]{2,1,0:T(2,128)S(1)} all-to-all(f32[32,2,16384]{2,1,0:T(2,128)S(1)} %pad_maximum_fusion.1), channel_id=1, replica_groups=mesh['det'=32,'tile'=8] {'det'}, dimensions={0} | all-to-all | bytes 8388608 | tf_op jit(solution)/shard_map/all_to_all | solution.py:117
  1002.5 3.8 fusion.18
  1006.4 0.7 bitcast_add_fusion
  (95 shorter events, 7.2 us)
Async XLA Ops:
  7.2 60.9 %copy-start = (f32[128,64]{0,1:T(8,128)S(1)}, f32[128,64]{0,1:T(8,128)}, u32[]{:S(2)}) copy-start(f32[128,64]{0,1:T(8,128)} %param.19) | copy-start | bytes 98308
  9.9 20.4 %all-to-all-start = ((s32[32,1,1]{2,1,0:T(1,128)}), s32[32,1,1]{2,1,0:T(1,128)S(1)}, u32[]{:S(2)}, u32[]{:S(2)}) async-start(s32[32,1,1]{2,1,0:T(1,128)} %copy.41), calls=%async_computation | async-start | bytes 32768 | tf_op jit(solution)/shard_map/all_to_all | solution.py:69
  32.5 5.2 copy-start.3
  32.5 5.5 copy-start.5
  33.7 28.3 %all-to-all-start.1 = ((bf16[32,128,128]{2,1,0:T(8,128)(2,1)}), bf16[32,128,128]{2,1,0:T(8,128)(2,1)S(1)}, u32[]{:S(2)}, u32[]{:S(2)}) async-start(bf16[32,128,128]{2,1,0:T(8,128)(2,1)} %select_select_fusion.1), calls=%async_computation.1 | async-start | bytes 2097152 | tf_op jit(solution)/shard_map/all_to_all | solution.py:80
  37.6 178.8 %all-reduce.3.cloned.1.call-start = ((), (), s32[]{:S(2)}) async-start(), calls=%async_computation.5 | async-start | bytes 2097152 | tf_op jit(solution)/shard_map/psum | solution.py:89
  62.0 6.0 copy-start.2
  68.0 2.4 copy-start.6
  68.0 148.4 %copy-start.4 = (f32[64,64]{1,0:T(8,128)S(1)}, f32[64,64]{1,0:T(8,128)}, u32[]{:S(2)}) copy-start(f32[64,64]{1,0:T(8,128)} %param.20) | copy-start | bytes 49156
  70.2 634.0 %all-reduce.5.cloned.1.call-start = ((), (), s32[]{:S(2)}) async-start(), calls=%async_computation.6 | async-start | bytes 2097152 | tf_op jit(solution)/shard_map/psum | solution.py:89
  514.5 3.9 copy-start.1
Sparse Core Ops, SparseCore 0:
  70.3 146.0 all-reduce.2
  561.0 143.1 all-reduce.4
where the time goes:
time: 1030 us; the launch traced here: 1010 us
  other arithmetic  368 us (36%)
  waiting for transfers between devices  320 us (31%)
  blocking collectives  262 us (25%)
  matrix products  24.3 us (2%)
  starting transfers between devices  15.9 us (2%)
  between operations  14.7 us (1%)
    psum x2, waiting for transfers between devices, local(): lax.psum(jnp.dot(my_templates.T, residual_signal, precision=lax.Precision...  289 us
    all_to_all x2, blocking collectives, local(): lax.all_to_all(stacked, 'det', split_axis=0, concat_axis=0, tiled=True)  195 us
    scatter-add x2, other arithmetic, local(): jnp.zeros((table_rows * PIX,), jnp.float32).at[flat_index]  175 us
    scatter-add x2, other arithmetic, local(): value_sums = jnp.zeros((table_rows * PIX,), jnp.float32).at[flat_index].a...  173 us
    psum x2, blocking collectives, local(): squares = lax.psum(jnp.sum(cleaned * cleaned, axis=1), 'tile')  34.1 us
    all_to_all x1, blocking collectives, local(): lax.all_to_all(outgoing, 'det', split_axis=0, concat_axis=0, tiled=True)  33.4 us
    all_to_all x1, waiting for transfers between devices, local(): lax.all_to_all(outgoing, 'det', split_axis=0, concat_axis=0, tiled=True)  23.9 us
  transfers between devices with their start and end apart: 4, of which 4 were waited for; matrix products, arithmetic and copies ran while one was open for 0% of the time, Pallas kernels for 0%

commit v1 on v0

v1 whole, which is shorter than its diff:
```python
import functools

import jax
import jax.numpy as jnp
from jax import lax
from jax.experimental import pallas as pl
from jax.experimental.pallas import tpu as pltpu
from jax.sharding import PartitionSpec as P

SIDE = 128
PIX = 16384
TILE_DEV = 2
MODES = 64
DETECTORS_LOCAL = 4
SAMP_DEV = 4096
SEG_PER = 4
BASELINE_COUNT = 16
ITERS = 2
PART = SAMP_DEV // SEG_PER
ENTRIES = DETECTORS_LOCAL * SEG_PER
LANES = 128
COLS = 256
ROWS = PIX * TILE_DEV // COLS

HUBER = 1.345
EPS = 1e-05
MESH = pl.DeviceIdType.MESH
ZRING = 8


def kernel(
    groups,
    blocks,
    ent_ref,
    own_ref,
    det_ref,
    code_ref,
    ends_ref,
    templ_ref,
    mixing_ref,
    sky_ref,
    sky_out,
    base_out,
    code_h,
    det_h,
    seg_h,
    code_e,
    val_e,
    work,
    clean_h,
    stack,
    matrix,
    current,
    acc,
    lhs,
    coloh,
    rowoh,
    send_i,
    recv_i,
    send_a,
    recv_a,
    send_b,
    recv_b,
    send_c,
    recv_c,
    send_d,
    recv_d,
    send_e,
    recv_e,
    sent,
    sem_i,
    sem_a,
    sem_b,
    sem_c,
    sem_d,
    sem_e,
):
    me = lax.axis_index("det")
    block = lax.axis_index("tile")
    chunks = SAMP_DEV // LANES
    xring = groups // ZRING
    my_x, my_z = me // ZRING, me % ZRING

    def peer(step):
        x = (my_x + step // ZRING) % xring
        z = (my_z + step % ZRING) % ZRING
        return x * ZRING + z

    def copy_to(src, dst, send_sem, recv_sem, **place):
        return pltpu.make_async_remote_copy(
            src_ref=src, dst_ref=dst, send_sem=send_sem, recv_sem=recv_sem,
            device_id=place, device_id_type=MESH,
        )

    def wait_bytes(ref, count, sem):
        view = ref.at[pl.ds(0, count)]
        pltpu.make_async_copy(view, view, sem).wait()

    barrier = pltpu.get_barrier_semaphore()

    def greet(step, carry):
        pl.semaphore_signal(barrier, inc=1, device_id={"det": peer(step)}, device_id_type=MESH)
        return carry

    lax.fori_loop(1, groups, greet, 0)

    def greet_tile(step, carry):
        pl.semaphore_signal(
            barrier, inc=1, device_id={"tile": (block + step) % blocks}, device_id_type=MESH
        )
        return carry

    lax.fori_loop(1, blocks, greet_tile, 0)

    det_h[...] = jnp.zeros_like(det_h)
    code_h[...] = jnp.zeros_like(code_h)
    clean_h[...] = jnp.zeros_like(clean_h)
    stack[...] = jnp.zeros_like(stack)
    for j in range(chunks):
        det_h[8 * j : 8 * j + DETECTORS_LOCAL, :] = det_ref[:, LANES * j : LANES * (j + 1)]
        code_h[8 * j : 8 * j + DETECTORS_LOCAL, :] = code_ref[:, LANES * j : LANES * (j + 1)]

    def entry_rows(e):
        l, k = e // SEG_PER, e % SEG_PER
        return pl.ds(8 * (PART // LANES) * k + l, PART // LANES, stride=8)

    for e in range(ENTRIES):
        code_e[e] = code_h[entry_rows(e), :]

    def pack_codes(o, carry):
        e = ent_ref[o]
        rows = code_e[jnp.maximum(e, 0)]
        send_i[o] = jnp.where(jnp.full(rows.shape, e, jnp.int32) >= 0, rows, -1)
        return carry

    lax.fori_loop(0, groups, pack_codes, 0)
    recv_i[me] = send_i[me]

    pl.semaphore_wait(barrier, groups - 1 + blocks - 1)

    def send_codes(step, carry):
        o = peer(step)
        copy_to(send_i.at[o], recv_i.at[me], sent.at[0], sem_i.at[me], det=o).start()
        return carry

    lax.fori_loop(1, groups, send_codes, 0)

    even = sky_ref[pl.ds(0, ROWS, stride=2), :]
    odd = sky_ref[pl.ds(1, ROWS, stride=2), :]
    current[:, 0:LANES] = even
    current[:, LANES:COLS] = odd
    mixed = jnp.dot(
        templ_ref[...], mixing_ref[...],
        precision=lax.Precision.HIGHEST, preferred_element_type=jnp.float32,
    )
    matrix[...] = lax.dot_general(
        mixed, templ_ref[...], (((1,), (1,)), ((), ())),
        precision=lax.Precision.HIGHEST, preferred_element_type=jnp.float32,
    )
    home = (chunks, 8, LANES)
    position = (
        lax.broadcasted_iota(jnp.int32, home, 0) * LANES + lax.broadcasted_iota(jnp.int32, home, 2)
    )
    ends = ends_ref[...]
    seg = jnp.zeros(home, jnp.int32)
    for n in range(BASELINE_COUNT):
        seg += (position >= ends[:, n : n + 1][None]).astype(jnp.int32)
    seg_h[...] = seg.reshape(8 * chunks, LANES)

    baseline = [jnp.zeros((8, 1), jnp.float32) for _ in range(BASELINE_COUNT)]

    for it in range(ITERS):
        base_sem = 1 + 5 * it
        table = current[...].astype(jnp.bfloat16)

        def answer(step, carry):
            d = peer(step)
            if it == 0:
                @pl.when(step > 0)
                def _():
                    copy_to(send_i.at[d], recv_i.at[d], sent.at[0], sem_i.at[d], det=d).wait_recv()

                code = recv_i[d]
                for q in range(PART // LANES):
                    here = pl.ds(LANES * q, LANES)
                    row = lax.shift_right_arithmetic(code[q : q + 1, :], 8)
                    col = jnp.bitwise_and(code[q : q + 1, :], COLS - 1)
                    coloh[d, :, here] = (
                        jnp.broadcast_to(col, (COLS, LANES))
                        == lax.broadcasted_iota(jnp.int32, (COLS, LANES), 0)
                    ).astype(jnp.float32).astype(jnp.bfloat16)
                    rowoh[d, :, here] = (
                        jnp.broadcast_to(row, (ROWS, LANES))
                        == lax.broadcasted_iota(jnp.int32, (ROWS, LANES), 0)
                    ).astype(jnp.float32).astype(jnp.bfloat16)
            picked = jnp.dot(table, coloh[d], preferred_element_type=jnp.float32)
            picked = jnp.sum(picked * rowoh[d].astype(jnp.float32), axis=0, keepdims=True)
            rows = jnp.concatenate(
                [picked[:, LANES * q : LANES * (q + 1)] for q in range(PART // LANES)], axis=0
            )
            send_a[it, d] = rows.astype(jnp.bfloat16)

            @pl.when(step > 0)
            def _():
                copy_to(
                    send_a.at[it, d], recv_a.at[it, me], sent.at[base_sem], sem_a.at[it], det=d
                ).start()

            return carry

        lax.fori_loop(0, groups, answer, 0)
        recv_a[it, me] = send_a[it, me]
        wait_bytes(recv_a.at[it], groups - 1, sem_a.at[it])

        for e in range(ENTRIES):
            work[entry_rows(e), :] = recv_a[it, own_ref[e]].astype(jnp.float32)
        residual = det_h[...] - work[...]
        det_h_value = residual
        for j in range(chunks):
            send_b[it, j] = det_h_value[8 * j : 8 * j + DETECTORS_LOCAL, :]
        recv_b[it, me] = send_b[it, me]

        def send_pieces(step, carry):
            j = peer(step)
            copy_to(
                send_b.at[it, j], recv_b.at[it, me], sent.at[base_sem + 1], sem_b.at[it], det=j
            ).start()
            return carry

        lax.fori_loop(1, groups, send_pieces, 0)
        wait_bytes(recv_b.at[it], groups - 1, sem_b.at[it])

        for d in range(groups):
            stack[8 * d : 8 * d + DETECTORS_LOCAL, :] = recv_b[it, d]
        every = stack[...]
        every = every - jnp.dot(
            matrix[...], every,
            precision=lax.Precision.HIGHEST, preferred_element_type=jnp.float32,
        )
        for d in range(groups):
            send_c[it, d] = every[8 * d : 8 * d + DETECTORS_LOCAL, :]
        recv_c[it, me] = send_c[it, me]

        def send_cleaned(step, carry):
            d = peer(step)
            copy_to(
                send_c.at[it, d], recv_c.at[it, me], sent.at[base_sem + 2], sem_c.at[it], det=d
            ).start()
            return carry

        lax.fori_loop(1, groups, send_cleaned, 0)
        wait_bytes(recv_c.at[it], groups - 1, sem_c.at[it])

        for j in range(chunks):
            clean_h[8 * j : 8 * j + DETECTORS_LOCAL, :] = recv_c[it, j]
        cleaned = clean_h[...].reshape(home)
        send_d[it] = jnp.sum(cleaned * cleaned, axis=0)
        recv_d[it, block] = send_d[it]

        def send_squares(step, carry):
            b = (block + step) % blocks
            copy_to(
                send_d.at[it], recv_d.at[it, block], sent.at[base_sem + 3], sem_d.at[it], tile=b
            ).start()
            return carry

        lax.fori_loop(1, blocks, send_squares, 0)
        wait_bytes(recv_d.at[it], blocks - 1, sem_d.at[it])
        squares = jnp.sum(jnp.sum(recv_d[it], axis=0), axis=1, keepdims=True)
        level = HUBER * jnp.sqrt(squares / (SAMP_DEV * blocks) + EPS)
        weight = level[None] / jnp.maximum(jnp.abs(cleaned), level[None])
        weighted = weight * cleaned
        seg = seg_h[...].reshape(home)
        stepped = jnp.zeros(home, jnp.float32)
        for n in range(BASELINE_COUNT):
            inside = seg == n
            numerator = jnp.sum(
                jnp.sum(jnp.where(inside, weighted, 0.0), axis=0), axis=1, keepdims=True
            )
            denominator = jnp.sum(
                jnp.sum(jnp.where(inside, weight, 0.0), axis=0), axis=1, keepdims=True
            )
            increment = numerator / jnp.where(denominator > 0.0, denominator, 1.0)
            baseline[n] = baseline[n] + increment
            stepped = jnp.where(inside, increment[None], stepped)
        if it + 1 < ITERS:
            det_h[...] = det_h[...] - stepped.reshape(8 * chunks, LANES)
        work[...] = (weight * (cleaned - stepped)).reshape(8 * chunks, LANES)
        clean_h[...] = weight.reshape(8 * chunks, LANES)
        half = PART // LANES
        for e in range(ENTRIES):
            val_e[e, 0:half, :] = work[entry_rows(e), :]
            val_e[e, half : 2 * half, :] = clean_h[entry_rows(e), :]

        def pack_values(o, carry):
            send_e[it, o] = val_e[jnp.maximum(ent_ref[o], 0)]
            return carry

        lax.fori_loop(0, groups, pack_values, 0)
        recv_e[it, me] = send_e[it, me]

        def send_values(step, carry):
            o = peer(step)
            copy_to(
                send_e.at[it, o], recv_e.at[it, me], sent.at[base_sem + 4], sem_e.at[it, me], det=o
            ).start()
            return carry

        lax.fori_loop(1, groups, send_values, 0)
        clean_h[...] = jnp.zeros_like(clean_h)
        acc[...] = jnp.zeros_like(acc)

        def collect(step, carry):
            d = peer(step)

            @pl.when(step > 0)
            def _():
                copy_to(
                    send_e.at[it, d], recv_e.at[it, d], sent.at[base_sem + 4], sem_e.at[it, d], det=d
                ).wait_recv()

            pair = recv_e[it, d]
            high = pair.astype(jnp.bfloat16).astype(jnp.float32)
            low = pair - high
            for q in range(half):
                here = pl.ds(LANES * q, LANES)
                flags = rowoh[d, :, here].astype(jnp.float32)
                for t, term in enumerate(
                    (high[q : q + 1], low[q : q + 1], high[half + q : half + q + 1],
                     low[half + q : half + q + 1])
                ):
                    lhs[ROWS * t : ROWS * (t + 1), here] = (
                        flags * jnp.broadcast_to(term, (ROWS, LANES))
                    ).astype(jnp.bfloat16)
            acc[...] += lax.dot_general(
                lhs[...], coloh[d], (((1,), (1,)), ((), ())), preferred_element_type=jnp.float32
            )
            return carry

        lax.fori_loop(0, groups, collect, 0)
        values = acc[0:ROWS, :] + acc[ROWS : 2 * ROWS, :]
        weights = acc[2 * ROWS : 3 * ROWS, :] + acc[3 * ROWS : 4 * ROWS, :]
        current[...] = current[...] + values / jnp.maximum(weights, 1.0)

    sky_out[pl.ds(0, ROWS, stride=2), :] = current[:, 0:LANES]
    sky_out[pl.ds(1, ROWS, stride=2), :] = current[:, LANES:COLS]
    lane = lax.broadcasted_iota(jnp.int32, (8, LANES), 1)
    fit = jnp.zeros((8, LANES), jnp.float32)
    for n in range(BASELINE_COUNT):
        fit = jnp.where(lane == n, baseline[n], fit)
    base_out[...] = fit

    wait_bytes(send_i, groups - 1, sent.at[0])
    for it in range(ITERS):
        base_sem = 1 + 5 * it
        wait_bytes(send_a.at[it], groups - 1, sent.at[base_sem])
        wait_bytes(send_b.at[it], groups - 1, sent.at[base_sem + 1])
        wait_bytes(send_c.at[it], groups - 1, sent.at[base_sem + 2])
        wait_bytes(recv_d.at[it], blocks - 1, sent.at[base_sem + 3])
        wait_bytes(send_e.at[it], groups - 1, sent.at[base_sem + 4])


def local(detector_samples, pixels, crossings, lengths, mode_templates, mixing, sky_map):
    groups = lax.axis_size("det")
    blocks = lax.axis_size("tile")
    chunks = SAMP_DEV // LANES
    tile_ids = crossings.reshape(ENTRIES)
    owner = tile_ids // TILE_DEV // blocks
    matches = owner[None, :] == jnp.arange(groups, dtype=jnp.int32)[:, None]
    entry = jnp.max(
        jnp.where(matches, jnp.arange(ENTRIES, dtype=jnp.int32)[None, :], -1), axis=1
    )
    local_tile = crossings.reshape(DETECTORS_LOCAL, SEG_PER) % TILE_DEV
    codes = (
        pixels.reshape(DETECTORS_LOCAL, SEG_PER, PART) + (local_tile * PIX)[:, :, None]
    ).reshape(DETECTORS_LOCAL, SAMP_DEV)
    ends = jnp.cumsum(lengths.reshape(DETECTORS_LOCAL, BASELINE_COUNT), axis=1)
    ends = jnp.pad(ends, ((0, 8 - DETECTORS_LOCAL), (0, LANES - BASELINE_COUNT)))
    templates = jnp.pad(
        mode_templates.reshape(groups, DETECTORS_LOCAL, MODES),
        ((0, 0), (0, 8 - DETECTORS_LOCAL), (0, 0)),
    ).reshape(groups * 8, MODES)

    vmem = pl.BlockSpec(memory_space=pltpu.VMEM)
    smem = pl.BlockSpec(memory_space=pltpu.SMEM)
    f32, bf16, i32 = jnp.float32, jnp.bfloat16, jnp.int32
    dma = pltpu.SemaphoreType.DMA
    half = PART // LANES
    sky, fit = pl.pallas_call(
        functools.partial(kernel, groups, blocks),
        out_shape=(
            jax.ShapeDtypeStruct((TILE_DEV * SIDE, SIDE), f32),
            jax.ShapeDtypeStruct((8, LANES), f32),
        ),
        in_specs=[smem, smem] + [vmem] * 6,
        out_specs=(vmem, vmem),
        scratch_shapes=[
            pltpu.VMEM((8 * chunks, LANES), i32),
            pltpu.VMEM((8 * chunks, LANES), f32),
            pltpu.VMEM((8 * chunks, LANES), i32),
            pltpu.VMEM((ENTRIES, half, LANES), i32),
            pltpu.VMEM((ENTRIES, 2 * half, LANES), f32),
            pltpu.VMEM((8 * chunks, LANES), f32),
            pltpu.VMEM((8 * chunks, LANES), f32),
            pltpu.VMEM((8 * groups, LANES), f32),
            pltpu.VMEM((8 * groups, 8 * groups), f32),
            pltpu.VMEM((ROWS, COLS), f32),
            pltpu.VMEM((4 * ROWS, COLS), f32),
            pltpu.VMEM((4 * ROWS, PART), bf16),
            pltpu.VMEM((groups, COLS, PART), bf16),
            pltpu.VMEM((groups, ROWS, PART), bf16),
            pltpu.VMEM((groups, half, LANES), i32),
            pltpu.VMEM((groups, half, LANES), i32),
            pltpu.VMEM((ITERS, groups, half, LANES), bf16),
            pltpu.VMEM((ITERS, groups, half, LANES), bf16),
            pltpu.VMEM((ITERS, chunks, DETECTORS_LOCAL, LANES), f32),
            pltpu.VMEM((ITERS, groups, DETECTORS_LOCAL, LANES), f32),
            pltpu.VMEM((ITERS, groups, DETECTORS_LOCAL, LANES), f32),
            pltpu.VMEM((ITERS, chunks, DETECTORS_LOCAL, LANES), f32),
            pltpu.VMEM((ITERS, 8, LANES), f32),
            pltpu.VMEM((ITERS, blocks, 8, LANES), f32),
            pltpu.VMEM((ITERS, groups, 2 * half, LANES), f32),
            pltpu.VMEM((ITERS, groups, 2 * half, LANES), f32),
            dma((1 + 5 * ITERS,)),
            dma((groups,)),
            dma((ITERS,)),
            dma((ITERS,)),
            dma((ITERS,)),
            dma((ITERS,)),
            dma((ITERS, groups)),
        ],
        compiler_params=pltpu.CompilerParams(
            collective_id=0, has_side_effects=True, vmem_limit_bytes=60 * 1024 * 1024
        ),
    )(entry, owner, detector_samples, codes, ends, templates, mixing,
      sky_map.reshape(TILE_DEV * SIDE, SIDE))
    return (
        sky.reshape(TILE_DEV, SIDE, SIDE),
        fit[:DETECTORS_LOCAL, :BASELINE_COUNT].reshape(DETECTORS_LOCAL, 1, BASELINE_COUNT),
    )


def solution(mesh):
    placed = (
        P("det", "tile"),
        P("det", "tile"),
        P("det", "tile", None),
        P("det", "tile", None),
        P(),
        P(),
        P(("det", "tile"), None, None),
    )
    return jax.shard_map(
        local,
        mesh=mesh,
        in_specs=placed,
        out_specs=(P(("det", "tile"), None, None), P("det", "tile", None)),
        check_vma=False,
    )
```

time: 1030 us -> 130 us (0.13); the launches traced: 1010 us -> 130 us
  other arithmetic: 368 us -> 2.11 us
  waiting for transfers between devices: 320 us -> 0 us
  blocking collectives: 262 us -> 0 us
  Pallas kernels: 0 us -> 121 us
  matrix products: 24.3 us -> 0 us
  starting transfers between devices: 15.9 us -> 0 us
  between operations: 14.7 us -> 0.69 us
    scatter-add x4 -> x0, other arithmetic: 348 us -> none  [the longest x2 175 us: local(): jnp.zeros((table_rows * PIX,), jnp.float32).at[flat_index]]
    psum x2 -> x0, waiting for transfers between devices: 289 us -> none  [local(): lax.psum(jnp.dot(my_templates.T, residual_signal, precision=lax.Precision...]
    all_to_all x3 -> x0, blocking collectives: 228 us -> none  [the longest x2 195 us: local(): lax.all_to_all(stacked, 'det', split_axis=0, concat_axis=0, tiled=True)]
    pallas_call x0 -> x1, Pallas kernels: none -> 121 us  [local(): pl.pallas_call(functools.partial(kernel, groups, blocks), out_shape=(jax....]
    psum x2 -> x0, blocking collectives: 34.1 us -> none  [local(): squares = lax.psum(jnp.sum(cleaned * cleaned, axis=1), 'tile')]
    all_to_all x2 -> x0, waiting for transfers between devices: 31.5 us -> none  [the longest x1 23.9 us: local(): lax.all_to_all(outgoing, 'det', split_axis=0, concat_axis=0, tiled=True)]
    dot_general x16 -> x0, matrix products: 24.3 us -> none  [the longest x2 7.62 us: local(): jnp.dot(chooser, arrived.reshape(groups, 2 * PIX), precision=lax.Precisio...]
    all_to_all x2 -> x0, starting transfers between devices: 15.8 us -> none  [the longest x1 11.9 us: local(): lax.all_to_all(wanted.reshape(groups, 1), 'det', split_axis=0, concat_axi...]
  transfers between devices with their start and end apart: 4 -> 0, of which waited for: 4 -> 0; matrix products, arithmetic and copies ran while one was open for 0% -> 0% of each run, Pallas kernels for 0% -> 0%
where the time goes in v1:
time: 130 us
  Pallas kernels  121 us (93%)
  local copies, waits for them, and re-layouts  6.01 us (5%)
  other arithmetic  2.11 us (2%)
    pallas_call x1, Pallas kernels, local(): pl.pallas_call(functools.partial(kernel, groups, blocks), out_shape=(jax....  121 us
    unnamed x17, local copies, waits for them, and re-layouts  4.08 us

profile of v1, /device:TPU:1, one launch (start us, length us, event | category | flops | bytes accessed | tf_op | source)
XLA Modules:
  0.0 129.8 jit_solution(3345248805884558707)
XLA Ops:
  0.6 0.0 copy-start.2
  0.6 0.5 broadcast.114
  1.2 0.2 copy-done.2
  1.3 0.7 reduce.3
  2.0 0.1 reshape.96
  2.1 0.0 copy-start.3
  2.1 0.0 copy-start.5
  2.1 0.6 select_reduce_fusion.ent_ref
  2.7 0.0 copy-done.5
  2.7 0.1 copy-done.3
  2.7 0.2 reduce_window_sum.11
  2.9 0.6 pad.8.ends_ref
  3.5 0.1 broadcast_bitcast_fusion
  3.6 0.0 copy-start
  3.7 0.8 copy-done
  4.5 0.0 copy-start.1
  4.5 0.6 add.38.code_ref
  5.1 0.1 copy-done.1
  5.2 0.1 copy.13
  5.3 0.7 pad_bitcast_fusion.templ_ref
  6.0 121.0 %shard_map.86 = (f32[256,128]{1,0:T(8,128)}, f32[8,128]{1,0:T(8,128)}) custom-call(s32[32]{0:T(128)} %select_reduce_fusion.ent_ref, s32[16]{0:T(128)} %copy-done.5, f32[4,4096]{1,0:T(4,128)} %det_ref.1, s32[4,4096]{1,0:T(4,128)} %add.38.code_ref, s32[8,128]{1,0:T(8,128)} %pad.8.ends_ref, f32[256,64]{1,0:T(8,128)} %pad_bitcast_fusion.templ_ref, ...), custom_call_target="tpu_custom_call" | custom-call | tf_op jit(solution)/shard_map/pallas_call | solution.py:389
  127.0 0.0 copy-start.4
  127.0 0.7 copy-done.4
  127.7 0.6 slice.3
  128.2 1.6 %copy.17 = f32[2,128,128]{2,1,0:T(8,128)} copy(f32[2,128,128]{2,1,0:T(8,128)} %bitcast.16) | data formatting | bytes 262144
  (3 shorter events, 0.1 us)
Async XLA Ops:
  0.6 0.7 copy-start.2
  2.1 0.7 copy-start.3
  2.1 0.6 copy-start.5
  3.6 0.8 copy-start
  4.5 0.8 copy-start.1
  127.0 0.7 copy-start.4

commit v2 on v1

v2 whole, which is shorter than its diff:
```python
import functools

import jax
import jax.numpy as jnp
from jax import lax
from jax.experimental import pallas as pl
from jax.experimental.pallas import tpu as pltpu
from jax.sharding import PartitionSpec as P

SIDE = 128
PIX = 16384
TILE_DEV = 2
MODES = 64
DETECTORS_LOCAL = 4
SAMP_DEV = 4096
SEG_PER = 4
BASELINE_COUNT = 16
ITERS = 2
PART = SAMP_DEV // SEG_PER
ENTRIES = DETECTORS_LOCAL * SEG_PER
LANES = 128
COLS = 256
ROWS = PIX // COLS
HALF = PART // LANES
TERMS = 3
TOGETHER = 4

HUBER = 1.345
EPS = 1e-05
MESH = pl.DeviceIdType.MESH
ZRING = 8


def kernel(
    groups,
    blocks,
    cross_ref,
    len_ref,
    det_hbm,
    pix_hbm,
    templ_hbm,
    mixing_hbm,
    sky_hbm,
    sky_out,
    base_out,
    det_ref,
    pix_ref,
    templ_ref,
    mixing_ref,
    current,
    ent_ref,
    templ_h,
    code_h,
    det_h,
    seg_h,
    code_e,
    val_e,
    work,
    clean_h,
    stack,
    matrix,
    table,
    chosen,
    parts,
    acc,
    coloh,
    rowoh,
    send_i,
    recv_i,
    send_a,
    recv_a,
    send_b,
    recv_b,
    send_c,
    recv_c,
    send_d,
    recv_d,
    send_e,
    recv_e,
    load_sem,
    sent,
    sem_i,
    sem_a,
    sem_b,
    sem_c,
    sem_d,
    sem_e,
):
    me = lax.axis_index("det")
    block = lax.axis_index("tile")
    chunks = SAMP_DEV // LANES
    xring = groups // ZRING
    my_x, my_z = lax.div(me, ZRING), lax.rem(me, ZRING)

    loads = [
        pltpu.make_async_copy(src, dst, load_sem.at[i])
        for i, (src, dst) in enumerate(
            ((pix_hbm, pix_ref), (det_hbm, det_ref), (templ_hbm, templ_ref),
             (mixing_hbm, mixing_ref), (sky_hbm, current))
        )
    ]
    for load in loads:
        load.start()

    def hops(dx, dz):
        return min(dx, xring - dx) + min(dz, ZRING - dz)

    xs = [lax.rem(my_x + dx, xring) * ZRING for dx in range(xring)]
    zs = [lax.rem(my_z + dz, ZRING) for dz in range(ZRING)]
    offsets = sorted(
        ((dx, dz) for dx in range(xring) for dz in range(ZRING) if dx or dz), key=lambda o: hops(*o)
    )
    near = [xs[dx] + zs[dz] for dx, dz in offsets]
    far = near[::-1]

    def copy_to(src, dst, send_sem, recv_sem, **place):
        return pltpu.make_async_remote_copy(
            src_ref=src, dst_ref=dst, send_sem=send_sem, recv_sem=recv_sem,
            device_id=place, device_id_type=MESH,
        )

    def wait_bytes(ref, count, sem):
        view = ref.at[pl.ds(0, count)]
        pltpu.make_async_copy(view, view, sem).wait()

    barrier = pltpu.get_barrier_semaphore()
    for o in far:
        pl.semaphore_signal(barrier, inc=1, device_id={"det": o}, device_id_type=MESH)
    others = [lax.rem(block + step, blocks) for step in range(1, blocks)]
    for b in others:
        pl.semaphore_signal(barrier, inc=1, device_id={"tile": b}, device_id_type=MESH)

    def entry_place(e):
        return e // SEG_PER, e % SEG_PER

    tiles = [cross_ref[entry_place(e)[0], 0, entry_place(e)[1]] for e in range(ENTRIES)]
    owners = [lax.div(tile, TILE_DEV * blocks) for tile in tiles]

    def find_entry(o, carry):
        found = jnp.int32(-1)
        for e in range(ENTRIES):
            found = jnp.where(owners[e] == o, e, found)
        ent_ref[o] = found
        return carry

    lax.fori_loop(0, groups, find_entry, 0)

    det_h[...] = jnp.zeros_like(det_h)
    code_h[...] = jnp.zeros_like(code_h)
    clean_h[...] = jnp.zeros_like(clean_h)
    stack[...] = jnp.zeros_like(stack)
    templ_h[...] = jnp.zeros_like(templ_h)
    loads[0].wait()
    for j in range(chunks):
        code_h[8 * j : 8 * j + DETECTORS_LOCAL, :] = pix_ref[:, LANES * j : LANES * (j + 1)]

    def entry_rows(e):
        l, k = entry_place(e)
        return pl.ds(8 * HALF * k + l, HALF, stride=8)

    for e in range(ENTRIES):
        code_e[e] = code_h[entry_rows(e), :] + lax.rem(tiles[e], TILE_DEV) * PIX

    def pack_codes(o, carry):
        e = ent_ref[o]
        rows = code_e[jnp.maximum(e, 0)]
        send_i[o] = jnp.where(jnp.full(rows.shape, e, jnp.int32) >= 0, rows, -1)
        return carry

    lax.fori_loop(0, groups, pack_codes, 0)
    recv_i[me] = send_i[me]
    for load in loads[1:]:
        load.wait()

    pl.semaphore_wait(barrier, groups - 1 + blocks - 1)
    for o in far:
        copy_to(send_i.at[o], recv_i.at[me], sent.at[0], sem_i.at[me], det=o).start()

    for j in range(chunks):
        det_h[8 * j : 8 * j + DETECTORS_LOCAL, :] = det_ref[:, LANES * j : LANES * (j + 1)]
    table[...] = current[...].astype(jnp.bfloat16).astype(jnp.float32)
    for d in range(groups):
        templ_h[8 * d : 8 * d + DETECTORS_LOCAL, :] = templ_ref[
            DETECTORS_LOCAL * d : DETECTORS_LOCAL * (d + 1), :
        ]
    mixed = jnp.dot(
        templ_h[...], mixing_ref[...],
        precision=lax.Precision.HIGHEST, preferred_element_type=jnp.float32,
    )
    matrix[...] = lax.dot_general(
        mixed, templ_h[...], (((1,), (1,)), ((), ())),
        precision=lax.Precision.HIGHEST, preferred_element_type=jnp.float32,
    )
    home = (chunks, 8, LANES)
    position = (
        lax.broadcasted_iota(jnp.int32, home, 0) * LANES + lax.broadcasted_iota(jnp.int32, home, 2)
    )
    sublane = lax.broadcasted_iota(jnp.int32, (8, LANES), 0)
    ends = [jnp.int32(0)] * DETECTORS_LOCAL
    seg = jnp.zeros(home, jnp.int32)
    for n in range(BASELINE_COUNT):
        end = jnp.zeros((8, LANES), jnp.int32)
        for l in range(DETECTORS_LOCAL):
            ends[l] = ends[l] + len_ref[l, 0, n]
            end = jnp.where(sublane == l, ends[l], end)
        seg += (position >= end[None]).astype(jnp.int32)
    seg_h[...] = seg.reshape(8 * chunks, LANES)

    def flags(first, last):
        def one(d, carry):
            code = recv_i[d]
            row = jnp.where(
                code < 0, -1, jnp.bitwise_and(lax.shift_right_arithmetic(code, 8), ROWS - 1)
            )
            col = jnp.bitwise_and(code, COLS - 1)
            for q in range(HALF):
                coloh[d, q] = (
                    jnp.broadcast_to(col[q : q + 1, :], (COLS, LANES))
                    == lax.broadcasted_iota(jnp.int32, (COLS, LANES), 0)
                ).astype(jnp.float32).astype(jnp.bfloat16)
                rowoh[d, q] = (
                    jnp.broadcast_to(row[q : q + 1, :], (ROWS, LANES))
                    == lax.broadcasted_iota(jnp.int32, (ROWS, LANES), 0)
                ).astype(jnp.float32).astype(jnp.bfloat16)
            return carry

        lax.fori_loop(first, last, one, 0)

    def peer_of(step):
        x = lax.rem(my_x + lax.div(step, ZRING), xring)
        z = lax.rem(my_z + lax.rem(step, ZRING), ZRING)
        return x * ZRING + z

    baseline = [jnp.zeros((8, 1), jnp.float32) for _ in range(BASELINE_COUNT)]

    for it in range(ITERS):
        base_sem = 1 + 5 * it

        def answer(batch, carry):
            slots = [
                peer_of(step if it == 0 else lax.rem(step + 20, groups))
                for step in (TOGETHER * batch + i for i in range(TOGETHER))
            ]
            if it == 0:
                for i, d in enumerate(slots):
                    @pl.when(TOGETHER * batch + i > 0)
                    def _():
                        copy_to(
                            send_i.at[d], recv_i.at[d], sent.at[0], sem_i.at[d], det=d
                        ).wait_recv()
            values = []
            for i, d in enumerate(slots):
                code = recv_i[d]
                row = jnp.bitwise_and(lax.shift_right_arithmetic(code, 7), SIDE - 1)
                col = jnp.bitwise_and(code, LANES - 1)
                second = code >= PIX
                for g in range(SIDE // 8):
                    chosen[i, 8 * g : 8 * g + 8, :] = jnp.where(
                        second,
                        table[SIDE + 8 * g : SIDE + 8 * g + 8, :],
                        table[8 * g : 8 * g + 8, :],
                    )
                value = jnp.zeros((HALF, LANES), jnp.float32)
                for r in range(SIDE):
                    line = jnp.broadcast_to(chosen[i, r : r + 1, :], (HALF, LANES))
                    value = jnp.where(row == r, jnp.take_along_axis(line, col, axis=1), value)
                values.append(value)
            for d, value in zip(slots, values):
                send_a[it, d] = value.astype(jnp.bfloat16)
            for d in slots:
                @pl.when(d != me)
                def _():
                    copy_to(
                        send_a.at[it, d], recv_a.at[it, me], sent.at[base_sem], sem_a.at[it], det=d
                    ).start()

            return carry

        lax.fori_loop(0, groups // TOGETHER, answer, 0)
        recv_a[it, me] = send_a[it, me]
        if it == 0:
            flags(0, groups // 2)
        wait_bytes(recv_a.at[it], groups - 1, sem_a.at[it])

        for e in range(ENTRIES):
            work[entry_rows(e), :] = recv_a[it, owners[e]].astype(jnp.float32)
        residual = det_h[...] - work[...]
        for j in range(chunks):
            send_b[it, j] = residual[8 * j : 8 * j + DETECTORS_LOCAL, :]
        recv_b[it, me] = send_b[it, me]
        for j in far:
            copy_to(
                send_b.at[it, j], recv_b.at[it, me], sent.at[base_sem + 1], sem_b.at[it], det=j
            ).start()
        if it == 0:
            flags(groups // 2, groups)
        wait_bytes(recv_b.at[it], groups - 1, sem_b.at[it])

        for d in range(groups):
            stack[8 * d : 8 * d + DETECTORS_LOCAL, :] = recv_b[it, d]
        every = stack[...]
        every = every - jnp.dot(
            matrix[...], every,
            precision=lax.Precision.HIGHEST, preferred_element_type=jnp.float32,
        )
        for d in range(groups):
            send_c[it, d] = every[8 * d : 8 * d + DETECTORS_LOCAL, :]
        recv_c[it, me] = send_c[it, me]
        for d in far:
            copy_to(
                send_c.at[it, d], recv_c.at[it, me], sent.at[base_sem + 2], sem_c.at[it], det=d
            ).start()
        acc[...] = jnp.zeros_like(acc)
        wait_bytes(recv_c.at[it], groups - 1, sem_c.at[it])

        for j in range(chunks):
            clean_h[8 * j : 8 * j + DETECTORS_LOCAL, :] = recv_c[it, j]
        cleaned = clean_h[...].reshape(home)
        send_d[it] = jnp.sum(cleaned * cleaned, axis=0)
        recv_d[it, block] = send_d[it]
        for b in others:
            copy_to(
                send_d.at[it], recv_d.at[it, block], sent.at[base_sem + 3], sem_d.at[it], tile=b
            ).start()
        wait_bytes(recv_d.at[it], blocks - 1, sem_d.at[it])
        squares = jnp.sum(jnp.sum(recv_d[it], axis=0), axis=1, keepdims=True)
        level = HUBER * jnp.sqrt(squares / (SAMP_DEV * blocks) + EPS)
        weight = level[None] / jnp.maximum(jnp.abs(cleaned), level[None])
        weighted = weight * cleaned
        seg = seg_h[...].reshape(home)
        stepped = jnp.zeros(home, jnp.float32)
        for n in range(BASELINE_COUNT):
            inside = seg == n
            numerator = jnp.sum(
                jnp.sum(jnp.where(inside, weighted, 0.0), axis=0), axis=1, keepdims=True
            )
            denominator = jnp.sum(
                jnp.sum(jnp.where(inside, weight, 0.0), axis=0), axis=1, keepdims=True
            )
            increment = numerator / jnp.where(denominator > 0.0, denominator, 1.0)
            baseline[n] = baseline[n] + increment
            stepped = jnp.where(inside, increment[None], stepped)
        if it + 1 < ITERS:
            det_h[...] = det_h[...] - stepped.reshape(8 * chunks, LANES)
        work[...] = (weight * (cleaned - stepped)).reshape(8 * chunks, LANES)
        clean_h[...] = weight.reshape(8 * chunks, LANES)
        for e in range(ENTRIES):
            value = work[entry_rows(e), :]
            high = value.astype(jnp.bfloat16)
            val_e[e, 0] = high
            val_e[e, 1] = (value - high.astype(jnp.float32)).astype(jnp.bfloat16)
            val_e[e, 2] = clean_h[entry_rows(e), :].astype(jnp.bfloat16)

        for o in far:
            send_e[it, o] = val_e[jnp.maximum(ent_ref[o], 0)]
            copy_to(
                send_e.at[it, o], recv_e.at[it, me], sent.at[base_sem + 4], sem_e.at[it, me], det=o
            ).start()
        recv_e[it, me] = val_e[jnp.maximum(ent_ref[me], 0)]
        clean_h[...] = jnp.zeros_like(clean_h)

        def collect(batch, carry):
            slots = [peer_of(TOGETHER * batch + i) for i in range(TOGETHER)]
            for i, d in enumerate(slots):
                @pl.when(TOGETHER * batch + i > 0)
                def _():
                    copy_to(
                        send_e.at[it, d], recv_e.at[it, d], sent.at[base_sem + 4], sem_e.at[it, d],
                        det=d,
                    ).wait_recv()
            for i, d in enumerate(slots):
                for t in range(TERMS):
                    parts[i, t] = recv_e[it, d, t].astype(jnp.float32)
            sums = []
            for i, d in enumerate(slots):
                weighed = jnp.concatenate(
                    [
                        jnp.concatenate(
                            [
                                rowoh[d, q]
                                * jnp.broadcast_to(
                                    parts[i, t, q : q + 1, :], (ROWS, LANES)
                                ).astype(jnp.bfloat16)
                                for t in range(TERMS)
                            ],
                            axis=0,
                        )
                        for q in range(HALF)
                    ],
                    axis=1,
                )
                columns = jnp.concatenate([coloh[d, q] for q in range(HALF)], axis=1)
                product = lax.dot_general(
                    weighed, columns, (((1,), (1,)), ((), ())), preferred_element_type=jnp.float32
                )
                second = jnp.broadcast_to(recv_i[d][0:1, 0:1], product.shape) >= PIX
                sums.append((jnp.where(second, 0.0, product), jnp.where(second, product, 0.0)))
            for t in range(TILE_DEV):
                total = sums[0][t]
                for part in sums[1:]:
                    total = total + part[t]
                acc[t] += total
            return carry

        lax.fori_loop(0, groups // TOGETHER, collect, 0)
        for t in range(TILE_DEV):
            change = (acc[t, 0:ROWS, :] + acc[t, ROWS : 2 * ROWS, :]) / jnp.maximum(
                acc[t, 2 * ROWS : 3 * ROWS, :], 1.0
            )
            for half in range(2):
                rows = pl.ds(SIDE * t + half, ROWS, stride=2)
                current[rows, :] = current[rows, :] + change[:, LANES * half : LANES * (half + 1)]
        if it + 1 < ITERS:
            table[...] = current[...].astype(jnp.bfloat16).astype(jnp.float32)

    sky_out[...] = current[...]
    lane = lax.broadcasted_iota(jnp.int32, (8, LANES), 1)
    fit = jnp.zeros((8, LANES), jnp.float32)
    for n in range(BASELINE_COUNT):
        fit = jnp.where(lane == n, baseline[n], fit)
    for l in range(DETECTORS_LOCAL):
        base_out[l] = fit[l : l + 1, 0:BASELINE_COUNT]

    wait_bytes(send_i, groups - 1, sent.at[0])
    for it in range(ITERS):
        base_sem = 1 + 5 * it
        wait_bytes(send_a.at[it], groups - 1, sent.at[base_sem])
        wait_bytes(send_b.at[it], groups - 1, sent.at[base_sem + 1])
        wait_bytes(send_c.at[it], groups - 1, sent.at[base_sem + 2])
        wait_bytes(recv_d.at[it], blocks - 1, sent.at[base_sem + 3])
        wait_bytes(send_e.at[it], groups - 1, sent.at[base_sem + 4])


def local(detector_samples, pixels, crossings, lengths, mode_templates, mixing, sky_map):
    groups = lax.axis_size("det")
    blocks = lax.axis_size("tile")
    chunks = SAMP_DEV // LANES
    vmem = pl.BlockSpec(memory_space=pltpu.VMEM)
    smem = pl.BlockSpec(memory_space=pltpu.SMEM)
    hbm = pl.BlockSpec(memory_space=pl.ANY)
    f32, bf16, i32 = jnp.float32, jnp.bfloat16, jnp.int32
    dma = pltpu.SemaphoreType.DMA
    sky, fit = pl.pallas_call(
        functools.partial(kernel, groups, blocks),
        out_shape=(
            jax.ShapeDtypeStruct((TILE_DEV * SIDE, SIDE), f32),
            jax.ShapeDtypeStruct((DETECTORS_LOCAL, 1, BASELINE_COUNT), f32),
        ),
        in_specs=[smem, smem] + [hbm] * 5,
        out_specs=(vmem, vmem),
        scratch_shapes=[
            pltpu.VMEM((DETECTORS_LOCAL, SAMP_DEV), f32),
            pltpu.VMEM((DETECTORS_LOCAL, SAMP_DEV), i32),
            pltpu.VMEM((DETECTORS_LOCAL * groups, MODES), f32),
            pltpu.VMEM((MODES, MODES), f32),
            pltpu.VMEM((TILE_DEV * SIDE, SIDE), f32),
            pltpu.SMEM((groups,), i32),
            pltpu.VMEM((8 * groups, MODES), f32),
            pltpu.VMEM((8 * chunks, LANES), i32),
            pltpu.VMEM((8 * chunks, LANES), f32),
            pltpu.VMEM((8 * chunks, LANES), i32),
            pltpu.VMEM((ENTRIES, HALF, LANES), i32),
            pltpu.VMEM((ENTRIES, TERMS, HALF, LANES), bf16),
            pltpu.VMEM((8 * chunks, LANES), f32),
            pltpu.VMEM((8 * chunks, LANES), f32),
            pltpu.VMEM((8 * groups, LANES), f32),
            pltpu.VMEM((8 * groups, 8 * groups), f32),
            pltpu.VMEM((TILE_DEV * SIDE, SIDE), f32),
            pltpu.VMEM((TOGETHER, SIDE, SIDE), f32),
            pltpu.VMEM((TOGETHER, TERMS, HALF, LANES), f32),
            pltpu.VMEM((TILE_DEV, TERMS * ROWS, COLS), f32),
            pltpu.VMEM((groups, HALF, COLS, LANES), bf16),
            pltpu.VMEM((groups, HALF, ROWS, LANES), bf16),
            pltpu.VMEM((groups, HALF, LANES), i32),
            pltpu.VMEM((groups, HALF, LANES), i32),
            pltpu.VMEM((ITERS, groups, HALF, LANES), bf16),
            pltpu.VMEM((ITERS, groups, HALF, LANES), bf16),
            pltpu.VMEM((ITERS, chunks, DETECTORS_LOCAL, LANES), f32),
            pltpu.VMEM((ITERS, groups, DETECTORS_LOCAL, LANES), f32),
            pltpu.VMEM((ITERS, groups, DETECTORS_LOCAL, LANES), f32),
            pltpu.VMEM((ITERS, chunks, DETECTORS_LOCAL, LANES), f32),
            pltpu.VMEM((ITERS, 8, LANES), f32),
            pltpu.VMEM((ITERS, blocks, 8, LANES), f32),
            pltpu.VMEM((ITERS, groups, TERMS, HALF, LANES), bf16),
            pltpu.VMEM((ITERS, groups, TERMS, HALF, LANES), bf16),
            dma((5,)),
            dma((1 + 5 * ITERS,)),
            dma((groups,)),
            dma((ITERS,)),
            dma((ITERS,)),
            dma((ITERS,)),
            dma((ITERS,)),
            dma((ITERS, groups)),
        ],
        compiler_params=pltpu.CompilerParams(
            collective_id=0, has_side_effects=True, vmem_limit_bytes=60 * 1024 * 1024
        ),
    )(crossings, lengths, detector_samples, pixels, mode_templates, mixing,
      sky_map.reshape(TILE_DEV * SIDE, SIDE))
    return sky.reshape(TILE_DEV, SIDE, SIDE), fit


def solution(mesh):
    placed = (
        P("det", "tile"),
        P("det", "tile"),
        P("det", "tile", None),
        P("det", "tile", None),
        P(),
        P(),
        P(("det", "tile"), None, None),
    )
    return jax.shard_map(
        local,
        mesh=mesh,
        in_specs=placed,
        out_specs=(P(("det", "tile"), None, None), P("det", "tile", None)),
        check_vma=False,
    )
```

time: 130 us -> 101 us (0.78)
  Pallas kernels: 121 us -> 96.4 us
  local copies, waits for them, and re-layouts: 6.01 us -> 3.64 us
  other arithmetic: 2.11 us -> 0 us
    pallas_call x1, Pallas kernels: 121 us -> 96.4 us  [local(): pl.pallas_call(functools.partial(kernel, groups, blocks), out_shape=(jax....]
    unnamed x17 -> x5, local copies, waits for them, and re-layouts: 4.08 us -> 3.64 us
where the time goes in v2:
time: 101 us
  Pallas kernels  96.4 us (95%)
  local copies, waits for them, and re-layouts  3.64 us (4%)
    pallas_call x1, Pallas kernels, local(): pl.pallas_call(functools.partial(kernel, groups, blocks), out_shape=(jax....  96.4 us
    unnamed x5, local copies, waits for them, and re-layouts  3.64 us

profile of v2, /device:TPU:1, one launch (start us, length us, event | category | flops | bytes accessed | tf_op | source)
XLA Modules:
  0.0 100.7 jit_solution(6643484002400745462)
XLA Ops:
  0.6 1.5 %copy.9.templ_hbm = f32[128,64]{1,0:T(8,128)} copy(f32[128,64]{0,1:T(8,128)} %param.11) | data formatting | bytes 65536 | tf_op args[4]
  2.1 96.4 %shard_map.86 = (f32[256,128]{1,0:T(8,128)}, f32[4,1,16]{2,1,0:T(1,128)}) custom-call(s32[4,1,4]{2,1,0:T(1,128)} %cross_ref.1, s32[4,1,16]{2,1,0:T(1,128)} %len_ref.1, f32[4,4096]{1,0:T(4,128)} %det_hbm.1, s32[4,4096]{1,0:T(4,128)} %pix_hbm.1, f32[128,64]{1,0:T(8,128)} %copy.9.templ_hbm, f32[64,64]{1,0:T(8,128)} %mixing_hbm.1, f32[256,128]{1,0:T(8,128)} %bitcast.3), custom_call_target="tpu_custom_call" | custom-call | tf_op jit(solution)/shard_map/pallas_call | solution.py:443
  98.6 0.0 copy-start
  98.6 1.6 %copy.12 = f32[2,128,128]{2,1,0:T(8,128)} copy(f32[2,128,128]{2,1,0:T(8,128)} %bitcast.2) | data formatting | bytes 262144
  100.1 0.0 copy-done
  100.1 0.6 copy.13
Async XLA Ops:
  98.6 1.6 %copy-start = (f32[4,1,16]{2,1,0:T(1,128)S(1)}, f32[4,1,16]{2,1,0:T(1,128)}, u32[]{:S(2)}) copy-start(f32[4,1,16]{2,1,0:T(1,128)} %get-tuple-element.9) | copy-start | bytes 772

commit v3 on v2

--- a/solution.py
+++ b/solution.py
@@ -24,6 +24,7 @@
 HALF = PART // LANES
 TERMS = 3
 TOGETHER = 4
+VMEM_BYTES = 32 * 1024 * 1024
 
 HUBER = 1.345
 EPS = 1e-05
@@ -34,8 +35,8 @@
 def kernel(
     groups,
     blocks,
-    cross_ref,
-    len_ref,
+    cross_hbm,
+    len_hbm,
     det_hbm,
     pix_hbm,
     templ_hbm,
@@ -43,6 +44,8 @@
     sky_hbm,
     sky_out,
     base_out,
+    cross_ref,
+    len_ref,
     det_ref,
     pix_ref,
     templ_ref,
@@ -63,6 +66,7 @@
     chosen,
     parts,
     acc,
+    columns,
     coloh,
     rowoh,
     send_i,
@@ -95,8 +99,8 @@
     loads = [
         pltpu.make_async_copy(src, dst, load_sem.at[i])
         for i, (src, dst) in enumerate(
-            ((pix_hbm, pix_ref), (det_hbm, det_ref), (templ_hbm, templ_ref),
-             (mixing_hbm, mixing_ref), (sky_hbm, current))
+            ((cross_hbm, cross_ref), (pix_hbm, pix_ref), (len_hbm, len_ref), (det_hbm, det_ref),
+             (templ_hbm, templ_ref), (mixing_hbm, mixing_ref), (sky_hbm, current))
         )
     ]
     for load in loads:
@@ -130,6 +134,7 @@
     for b in others:
         pl.semaphore_signal(barrier, inc=1, device_id={"tile": b}, device_id_type=MESH)
 
+    loads[0].wait()
     def entry_place(e):
         return e // SEG_PER, e % SEG_PER
 
@@ -150,7 +155,7 @@
     clean_h[...] = jnp.zeros_like(clean_h)
     stack[...] = jnp.zeros_like(stack)
     templ_h[...] = jnp.zeros_like(templ_h)
-    loads[0].wait()
+    loads[1].wait()
     for j in range(chunks):
         code_h[8 * j : 8 * j + DETECTORS_LOCAL, :] = pix_ref[:, LANES * j : LANES * (j + 1)]
 
@@ -169,18 +174,19 @@
 
     lax.fori_loop(0, groups, pack_codes, 0)
     recv_i[me] = send_i[me]
-    for load in loads[1:]:
+    for load in loads[2:]:
         load.wait()
 
     pl.semaphore_wait(barrier, groups - 1 + blocks - 1)
-    for o in far:
+    for o in near:
         copy_to(send_i.at[o], recv_i.at[me], sent.at[0], sem_i.at[me], det=o).start()
 
     for j in range(chunks):
         det_h[8 * j : 8 * j + DETECTORS_LOCAL, :] = det_ref[:, LANES * j : LANES * (j + 1)]
     table[...] = current[...].astype(jnp.bfloat16).astype(jnp.float32)
+    templates = templ_ref[...].T
     for d in range(groups):
-        templ_h[8 * d : 8 * d + DETECTORS_LOCAL, :] = templ_ref[
+        templ_h[8 * d : 8 * d + DETECTORS_LOCAL, :] = templates[
             DETECTORS_LOCAL * d : DETECTORS_LOCAL * (d + 1), :
         ]
     mixed = jnp.dot(
@@ -206,25 +212,37 @@
         seg += (position >= end[None]).astype(jnp.int32)
     seg_h[...] = seg.reshape(8 * chunks, LANES)
 
-    def flags(first, last):
-        def one(d, carry):
+    def turn_columns():
+        column = jnp.bitwise_and(recv_i[...].reshape(groups * HALF, LANES), COLS - 1).T
+        for part in range(groups * HALF // LANES):
+            columns[part] = column[:, LANES * part : LANES * (part + 1)]
+
+    def flags(part):
+        slots = LANES // HALF
+
+        def one(i, carry):
+            d = slots * part + i
             code = recv_i[d]
             row = jnp.where(
                 code < 0, -1, jnp.bitwise_and(lax.shift_right_arithmetic(code, 8), ROWS - 1)
             )
-            col = jnp.bitwise_and(code, COLS - 1)
+            square = (LANES, LANES)
+            lane = lax.broadcasted_iota(jnp.int32, square, 1)
             for q in range(HALF):
-                coloh[d, q] = (
-                    jnp.broadcast_to(col[q : q + 1, :], (COLS, LANES))
-                    == lax.broadcasted_iota(jnp.int32, (COLS, LANES), 0)
-                ).astype(jnp.float32).astype(jnp.bfloat16)
                 rowoh[d, q] = (
                     jnp.broadcast_to(row[q : q + 1, :], (ROWS, LANES))
                     == lax.broadcasted_iota(jnp.int32, (ROWS, LANES), 0)
                 ).astype(jnp.float32).astype(jnp.bfloat16)
+                col = jnp.take_along_axis(
+                    columns[part], jnp.full(square, HALF * i + q, jnp.int32), axis=1
+                )
+                for h in range(COLS // LANES):
+                    coloh[d, h, LANES * q : LANES * (q + 1), :] = (
+                        col == lane + LANES * h
+                    ).astype(jnp.float32).astype(jnp.bfloat16)
             return carry
 
-        lax.fori_loop(first, last, one, 0)
+        lax.fori_loop(0, slots, one, 0)
 
     def peer_of(step):
         x = lax.rem(my_x + lax.div(step, ZRING), xring)
@@ -279,7 +297,8 @@
         lax.fori_loop(0, groups // TOGETHER, answer, 0)
         recv_a[it, me] = send_a[it, me]
         if it == 0:
-            flags(0, groups // 2)
+            turn_columns()
+            flags(0)
         wait_bytes(recv_a.at[it], groups - 1, sem_a.at[it])
 
         for e in range(ENTRIES):
@@ -293,7 +312,7 @@
                 send_b.at[it, j], recv_b.at[it, me], sent.at[base_sem + 1], sem_b.at[it], det=j
             ).start()
         if it == 0:
-            flags(groups // 2, groups)
+            flags(1)
         wait_bytes(recv_b.at[it], groups - 1, sem_b.at[it])
 
         for d in range(groups):
@@ -351,7 +370,7 @@
             val_e[e, 1] = (value - high.astype(jnp.float32)).astype(jnp.bfloat16)
             val_e[e, 2] = clean_h[entry_rows(e), :].astype(jnp.bfloat16)
 
-        for o in far:
+        for o in near:
             send_e[it, o] = val_e[jnp.maximum(ent_ref[o], 0)]
             copy_to(
                 send_e.at[it, o], recv_e.at[it, me], sent.at[base_sem + 4], sem_e.at[it, me], det=o
@@ -389,10 +408,8 @@
                     ],
                     axis=1,
                 )
-                columns = jnp.concatenate([coloh[d, q] for q in range(HALF)], axis=1)
-                product = lax.dot_general(
-                    weighed, columns, (((1,), (1,)), ((), ())), preferred_element_type=jnp.float32
-                )
+                spread = jnp.concatenate([coloh[d, h] for h in range(COLS // LANES)], axis=1)
+                product = jnp.dot(weighed, spread, preferred_element_type=jnp.float32)
                 second = jnp.broadcast_to(recv_i[d][0:1, 0:1], product.shape) >= PIX
                 sums.append((jnp.where(second, 0.0, product), jnp.where(second, product, 0.0)))
             for t in range(TILE_DEV):
@@ -436,8 +453,7 @@
     blocks = lax.axis_size("tile")
     chunks = SAMP_DEV // LANES
     vmem = pl.BlockSpec(memory_space=pltpu.VMEM)
-    smem = pl.BlockSpec(memory_space=pltpu.SMEM)
-    hbm = pl.BlockSpec(memory_space=pl.ANY)
+    hbm = pl.BlockSpec(memory_space=pltpu.HBM)
     f32, bf16, i32 = jnp.float32, jnp.bfloat16, jnp.int32
     dma = pltpu.SemaphoreType.DMA
     sky, fit = pl.pallas_call(
@@ -446,12 +462,14 @@
             jax.ShapeDtypeStruct((TILE_DEV * SIDE, SIDE), f32),
             jax.ShapeDtypeStruct((DETECTORS_LOCAL, 1, BASELINE_COUNT), f32),
         ),
-        in_specs=[smem, smem] + [hbm] * 5,
+        in_specs=[hbm] * 7,
         out_specs=(vmem, vmem),
         scratch_shapes=[
+            pltpu.SMEM((DETECTORS_LOCAL, 1, SEG_PER), i32),
+            pltpu.SMEM((DETECTORS_LOCAL, 1, BASELINE_COUNT), i32),
             pltpu.VMEM((DETECTORS_LOCAL, SAMP_DEV), f32),
             pltpu.VMEM((DETECTORS_LOCAL, SAMP_DEV), i32),
-            pltpu.VMEM((DETECTORS_LOCAL * groups, MODES), f32),
+            pltpu.VMEM((MODES, DETECTORS_LOCAL * groups), f32),
             pltpu.VMEM((MODES, MODES), f32),
             pltpu.VMEM((TILE_DEV * SIDE, SIDE), f32),
             pltpu.SMEM((groups,), i32),
@@ -469,7 +487,8 @@
             pltpu.VMEM((TOGETHER, SIDE, SIDE), f32),
             pltpu.VMEM((TOGETHER, TERMS, HALF, LANES), f32),
             pltpu.VMEM((TILE_DEV, TERMS * ROWS, COLS), f32),
-            pltpu.VMEM((groups, HALF, COLS, LANES), bf16),
+            pltpu.VMEM((groups * HALF // LANES, LANES, LANES), i32),
+            pltpu.VMEM((groups, COLS // LANES, PART, LANES), bf16),
             pltpu.VMEM((groups, HALF, ROWS, LANES), bf16),
             pltpu.VMEM((groups, HALF, LANES), i32),
             pltpu.VMEM((groups, HALF, LANES), i32),
@@ -483,7 +502,7 @@
             pltpu.VMEM((ITERS, blocks, 8, LANES), f32),
             pltpu.VMEM((ITERS, groups, TERMS, HALF, LANES), bf16),
             pltpu.VMEM((ITERS, groups, TERMS, HALF, LANES), bf16),
-            dma((5,)),
+            dma((7,)),
             dma((1 + 5 * ITERS,)),
             dma((groups,)),
             dma((ITERS,)),
@@ -493,10 +512,15 @@
             dma((ITERS, groups)),
         ],
         compiler_params=pltpu.CompilerParams(
-            collective_id=0, has_side_effects=True, vmem_limit_bytes=60 * 1024 * 1024
+            collective_id=0, has_side_effects=True, vmem_limit_bytes=VMEM_BYTES
         ),
-    )(crossings, lengths, detector_samples, pixels, mode_templates, mixing,
-      sky_map.reshape(TILE_DEV * SIDE, SIDE))
+    )(*(
+        pltpu.with_memory_space_constraint(array, pltpu.HBM)
+        for array in (
+            crossings, lengths, detector_samples, pixels, mode_templates.T, mixing,
+            sky_map.reshape(TILE_DEV * SIDE, SIDE),
+        )
+    ))
     return sky.reshape(TILE_DEV, SIDE, SIDE), fit
 
 

time: 101 us -> 91.8 us (0.909); the launches traced: 101 us -> 90.5 us
  Pallas kernels: 96.4 us -> 88.6 us
  local copies, waits for them, and re-layouts: 3.64 us -> 1.24 us
    pallas_call x1, Pallas kernels: 96.4 us -> 88.6 us  [local(): pl.pallas_call(functools.partial(kernel, groups, blocks), out_shape=(jax....]
    unnamed x5 -> x2, local copies, waits for them, and re-layouts: 3.64 us -> 1.24 us
where the time goes in v3:
time: 91.8 us; the launch traced here: 90.5 us
  Pallas kernels  88.6 us (97%)
  local copies, waits for them, and re-layouts  1.24 us (1%)
    pallas_call x1, Pallas kernels, local(): pl.pallas_call(functools.partial(kernel, groups, blocks), out_shape=(jax....  88.6 us

profile of v3, /device:TPU:1, one launch (start us, length us, event | category | flops | bytes accessed | tf_op | source)
XLA Modules:
  0.0 90.5 jit_solution(2568318588482947634)
XLA Ops:
  0.6 88.6 %shard_map.86 = (f32[256,128]{1,0:T(8,128)S(1)}, f32[4,1,16]{2,1,0:T(1,128)S(1)}) custom-call(s32[4,1,4]{2,1,0:T(1,128)} %cross_hbm.1, s32[4,1,16]{2,1,0:T(1,128)} %len_hbm.1, f32[4,4096]{1,0:T(4,128)} %det_hbm.1, s32[4,4096]{1,0:T(4,128)} %pix_hbm.1, f32[64,128]{1,0:T(8,128)} %bitcast.5, f32[64,64]{1,0:T(8,128)} %mixing_hbm.1, f32[256,128]{1,0:T(8,128)} %bitcast.4), custom_call_target="tpu_custom_call" | custom-call | tf_op jit(solution)/shard_map/pallas_call | solution.py:459
  89.3 0.7 copy.11
  89.9 0.6 copy.12

commit v4 on v3

--- a/solution.py
+++ b/solution.py
@@ -23,6 +23,8 @@
 ROWS = PIX // COLS
 HALF = PART // LANES
 TERMS = 3
+SEG_BITS = 16
+SEG_UNIT = 1 << SEG_BITS
 TOGETHER = 4
 VMEM_BYTES = 32 * 1024 * 1024
 
@@ -81,6 +83,9 @@
     recv_d,
     send_e,
     recv_e,
+    head,
+    send_h,
+    recv_h,
     load_sem,
     sent,
     sem_i,
@@ -89,6 +94,7 @@
     sem_c,
     sem_d,
     sem_e,
+    sem_h,
 ):
     me = lax.axis_index("det")
     block = lax.axis_index("tile")
@@ -159,12 +165,32 @@
     for j in range(chunks):
         code_h[8 * j : 8 * j + DETECTORS_LOCAL, :] = pix_ref[:, LANES * j : LANES * (j + 1)]
 
+    loads[2].wait()
+    home = (chunks, 8, LANES)
+    position = (
+        lax.broadcasted_iota(jnp.int32, home, 0) * LANES + lax.broadcasted_iota(jnp.int32, home, 2)
+    )
+    sublane = lax.broadcasted_iota(jnp.int32, (8, LANES), 0)
+    ends = [jnp.int32(0)] * DETECTORS_LOCAL
+    seg = jnp.zeros(home, jnp.int32)
+    for n in range(BASELINE_COUNT):
+        end = jnp.zeros((8, LANES), jnp.int32)
+        for l in range(DETECTORS_LOCAL):
+            ends[l] = ends[l] + len_ref[l, 0, n]
+            end = jnp.where(sublane == l, ends[l], end)
+        seg += (position >= end[None]).astype(jnp.int32)
+    seg_h[...] = seg.reshape(8 * chunks, LANES)
+
     def entry_rows(e):
         l, k = entry_place(e)
         return pl.ds(8 * HALF * k + l, HALF, stride=8)
 
     for e in range(ENTRIES):
-        code_e[e] = code_h[entry_rows(e), :] + lax.rem(tiles[e], TILE_DEV) * PIX
+        code_e[e] = (
+            code_h[entry_rows(e), :]
+            + lax.rem(tiles[e], TILE_DEV) * PIX
+            + seg_h[entry_rows(e), :] * SEG_UNIT
+        )
 
     def pack_codes(o, carry):
         e = ent_ref[o]
@@ -174,7 +200,7 @@
 
     lax.fori_loop(0, groups, pack_codes, 0)
     recv_i[me] = send_i[me]
-    for load in loads[2:]:
+    for load in loads[3:]:
         load.wait()
 
     pl.semaphore_wait(barrier, groups - 1 + blocks - 1)
@@ -197,21 +223,6 @@
         mixed, templ_h[...], (((1,), (1,)), ((), ())),
         precision=lax.Precision.HIGHEST, preferred_element_type=jnp.float32,
     )
-    home = (chunks, 8, LANES)
-    position = (
-        lax.broadcasted_iota(jnp.int32, home, 0) * LANES + lax.broadcasted_iota(jnp.int32, home, 2)
-    )
-    sublane = lax.broadcasted_iota(jnp.int32, (8, LANES), 0)
-    ends = [jnp.int32(0)] * DETECTORS_LOCAL
-    seg = jnp.zeros(home, jnp.int32)
-    for n in range(BASELINE_COUNT):
-        end = jnp.zeros((8, LANES), jnp.int32)
-        for l in range(DETECTORS_LOCAL):
-            ends[l] = ends[l] + len_ref[l, 0, n]
-            end = jnp.where(sublane == l, ends[l], end)
-        seg += (position >= end[None]).astype(jnp.int32)
-    seg_h[...] = seg.reshape(8 * chunks, LANES)
-
     def turn_columns():
         column = jnp.bitwise_and(recv_i[...].reshape(groups * HALF, LANES), COLS - 1).T
         for part in range(groups * HALF // LANES):
@@ -252,7 +263,7 @@
     baseline = [jnp.zeros((8, 1), jnp.float32) for _ in range(BASELINE_COUNT)]
 
     for it in range(ITERS):
-        base_sem = 1 + 5 * it
+        base_sem = 1 + 6 * it
 
         def answer(batch, carry):
             slots = [
@@ -271,7 +282,7 @@
                 code = recv_i[d]
                 row = jnp.bitwise_and(lax.shift_right_arithmetic(code, 7), SIDE - 1)
                 col = jnp.bitwise_and(code, LANES - 1)
-                second = code >= PIX
+                second = jnp.bitwise_and(code, PIX) > 0
                 for g in range(SIDE // 8):
                     chosen[i, 8 * g : 8 * g + 8, :] = jnp.where(
                         second,
@@ -341,13 +352,23 @@
             copy_to(
                 send_d.at[it], recv_d.at[it, block], sent.at[base_sem + 3], sem_d.at[it], tile=b
             ).start()
+        for e in range(ENTRIES):
+            val_e[e] = clean_h[entry_rows(e), :]
+        for o in near:
+            send_e[it, o] = val_e[jnp.maximum(ent_ref[o], 0)]
+            copy_to(
+                send_e.at[it, o], recv_e.at[it, me], sent.at[base_sem + 4], sem_e.at[it, me], det=o
+            ).start()
+        recv_e[it, me] = val_e[jnp.maximum(ent_ref[me], 0)]
         wait_bytes(recv_d.at[it], blocks - 1, sem_d.at[it])
         squares = jnp.sum(jnp.sum(recv_d[it], axis=0), axis=1, keepdims=True)
         level = HUBER * jnp.sqrt(squares / (SAMP_DEV * blocks) + EPS)
         weight = level[None] / jnp.maximum(jnp.abs(cleaned), level[None])
         weighted = weight * cleaned
         seg = seg_h[...].reshape(home)
-        stepped = jnp.zeros(home, jnp.float32)
+        lane = lax.broadcasted_iota(jnp.int32, (8, LANES), 1)
+        line = jnp.where(lane == BASELINE_COUNT, level, 0.0)
+        increments = []
         for n in range(BASELINE_COUNT):
             inside = seg == n
             numerator = jnp.sum(
@@ -357,26 +378,23 @@
                 jnp.sum(jnp.where(inside, weight, 0.0), axis=0), axis=1, keepdims=True
             )
             increment = numerator / jnp.where(denominator > 0.0, denominator, 1.0)
-            baseline[n] = baseline[n] + increment
-            stepped = jnp.where(inside, increment[None], stepped)
+            increments.append(increment)
+            line = jnp.where(lane == n, increment, line)
+        for l in range(DETECTORS_LOCAL):
+            head[l] = line[l : l + 1, :]
+        for o in near:
+            send_h[it, o] = head[lax.div(jnp.maximum(ent_ref[o], 0), SEG_PER)]
+            copy_to(
+                send_h.at[it, o], recv_h.at[it, me], sent.at[base_sem + 5], sem_h.at[it, me], det=o
+            ).start()
+        recv_h[it, me] = head[lax.div(jnp.maximum(ent_ref[me], 0), SEG_PER)]
+        for n in range(BASELINE_COUNT):
+            baseline[n] = baseline[n] + increments[n]
         if it + 1 < ITERS:
+            stepped = jnp.zeros(home, jnp.float32)
+            for n in range(BASELINE_COUNT):
+                stepped = jnp.where(seg == n, increments[n][None], stepped)
             det_h[...] = det_h[...] - stepped.reshape(8 * chunks, LANES)
-        work[...] = (weight * (cleaned - stepped)).reshape(8 * chunks, LANES)
-        clean_h[...] = weight.reshape(8 * chunks, LANES)
-        for e in range(ENTRIES):
-            value = work[entry_rows(e), :]
-            high = value.astype(jnp.bfloat16)
-            val_e[e, 0] = high
-            val_e[e, 1] = (value - high.astype(jnp.float32)).astype(jnp.bfloat16)
-            val_e[e, 2] = clean_h[entry_rows(e), :].astype(jnp.bfloat16)
-
-        for o in near:
-            send_e[it, o] = val_e[jnp.maximum(ent_ref[o], 0)]
-            copy_to(
-                send_e.at[it, o], recv_e.at[it, me], sent.at[base_sem + 4], sem_e.at[it, me], det=o
-            ).start()
-        recv_e[it, me] = val_e[jnp.maximum(ent_ref[me], 0)]
-        clean_h[...] = jnp.zeros_like(clean_h)
 
         def collect(batch, carry):
             slots = [peer_of(TOGETHER * batch + i) for i in range(TOGETHER)]
@@ -387,9 +405,26 @@
                         send_e.at[it, d], recv_e.at[it, d], sent.at[base_sem + 4], sem_e.at[it, d],
                         det=d,
                     ).wait_recv()
+                    copy_to(
+                        send_h.at[it, d], recv_h.at[it, d], sent.at[base_sem + 5], sem_h.at[it, d],
+                        det=d,
+                    ).wait_recv()
             for i, d in enumerate(slots):
-                for t in range(TERMS):
-                    parts[i, t] = recv_e[it, d, t].astype(jnp.float32)
+                cleaned_d = recv_e[it, d]
+                line = jnp.broadcast_to(recv_h[it, d], (HALF, LANES))
+                seg_d = jnp.bitwise_and(
+                    lax.shift_right_arithmetic(recv_i[d], SEG_BITS), BASELINE_COUNT - 1
+                )
+                step_d = jnp.take_along_axis(line, seg_d, axis=1)
+                level_d = jnp.take_along_axis(
+                    line, jnp.full((HALF, LANES), BASELINE_COUNT, jnp.int32), axis=1
+                )
+                weight_d = level_d / jnp.maximum(jnp.abs(cleaned_d), level_d)
+                value_d = weight_d * (cleaned_d - step_d)
+                high = value_d.astype(jnp.bfloat16).astype(jnp.float32)
+                parts[i, 0] = high
+                parts[i, 1] = value_d - high
+                parts[i, 2] = weight_d
             sums = []
             for i, d in enumerate(slots):
                 weighed = jnp.concatenate(
@@ -410,7 +445,9 @@
                 )
                 spread = jnp.concatenate([coloh[d, h] for h in range(COLS // LANES)], axis=1)
                 product = jnp.dot(weighed, spread, preferred_element_type=jnp.float32)
-                second = jnp.broadcast_to(recv_i[d][0:1, 0:1], product.shape) >= PIX
+                second = (
+                    jnp.broadcast_to(jnp.bitwise_and(recv_i[d], PIX)[0:1, 0:1], product.shape) > 0
+                )
                 sums.append((jnp.where(second, 0.0, product), jnp.where(second, product, 0.0)))
             for t in range(TILE_DEV):
                 total = sums[0][t]
@@ -440,12 +477,13 @@
 
     wait_bytes(send_i, groups - 1, sent.at[0])
     for it in range(ITERS):
-        base_sem = 1 + 5 * it
+        base_sem = 1 + 6 * it
         wait_bytes(send_a.at[it], groups - 1, sent.at[base_sem])
         wait_bytes(send_b.at[it], groups - 1, sent.at[base_sem + 1])
         wait_bytes(send_c.at[it], groups - 1, sent.at[base_sem + 2])
         wait_bytes(recv_d.at[it], blocks - 1, sent.at[base_sem + 3])
         wait_bytes(send_e.at[it], groups - 1, sent.at[base_sem + 4])
+        wait_bytes(send_h.at[it], groups - 1, sent.at[base_sem + 5])
 
 
 def local(detector_samples, pixels, crossings, lengths, mode_templates, mixing, sky_map):
@@ -478,7 +516,7 @@
             pltpu.VMEM((8 * chunks, LANES), f32),
             pltpu.VMEM((8 * chunks, LANES), i32),
             pltpu.VMEM((ENTRIES, HALF, LANES), i32),
-            pltpu.VMEM((ENTRIES, TERMS, HALF, LANES), bf16),
+            pltpu.VMEM((ENTRIES, HALF, LANES), f32),
             pltpu.VMEM((8 * chunks, LANES), f32),
             pltpu.VMEM((8 * chunks, LANES), f32),
             pltpu.VMEM((8 * groups, LANES), f32),
@@ -500,15 +538,19 @@
             pltpu.VMEM((ITERS, chunks, DETECTORS_LOCAL, LANES), f32),
             pltpu.VMEM((ITERS, 8, LANES), f32),
             pltpu.VMEM((ITERS, blocks, 8, LANES), f32),
-            pltpu.VMEM((ITERS, groups, TERMS, HALF, LANES), bf16),
-            pltpu.VMEM((ITERS, groups, TERMS, HALF, LANES), bf16),
+            pltpu.VMEM((ITERS, groups, HALF, LANES), f32),
+            pltpu.VMEM((ITERS, groups, HALF, LANES), f32),
+            pltpu.VMEM((DETECTORS_LOCAL, 1, LANES), f32),
+            pltpu.VMEM((ITERS, groups, 1, LANES), f32),
+            pltpu.VMEM((ITERS, groups, 1, LANES), f32),
             dma((7,)),
-            dma((1 + 5 * ITERS,)),
+            dma((1 + 6 * ITERS,)),
             dma((groups,)),
             dma((ITERS,)),
             dma((ITERS,)),
             dma((ITERS,)),
             dma((ITERS,)),
+            dma((ITERS, groups)),
             dma((ITERS, groups)),
         ],
         compiler_params=pltpu.CompilerParams(

time: 91.8 us -> 89 us (0.969); the launches traced: 90.5 us -> 88.9 us
  Pallas kernels: 88.6 us -> 87 us
    pallas_call x1, Pallas kernels: 88.6 us -> 87 us  [local(): pl.pallas_call(functools.partial(kernel, groups, blocks), out_shape=(jax....]
where the time goes in v4:
time: 89 us; the launch traced here: 88.9 us
  Pallas kernels  87 us (98%)
  local copies, waits for them, and re-layouts  1.24 us (1%)
    pallas_call x1, Pallas kernels, local(): pl.pallas_call(functools.partial(kernel, groups, blocks), out_shape=(jax....  87 us

profile of v4, /device:TPU:1, one launch (start us, length us, event | category | flops | bytes accessed | tf_op | source)
XLA Modules:
  0.0 88.9 jit_solution(6557639766410728306)
XLA Ops:
  0.6 87.0 %shard_map.86 = (f32[256,128]{1,0:T(8,128)S(1)}, f32[4,1,16]{2,1,0:T(1,128)S(1)}) custom-call(s32[4,1,4]{2,1,0:T(1,128)} %cross_hbm.1, s32[4,1,16]{2,1,0:T(1,128)} %len_hbm.1, f32[4,4096]{1,0:T(4,128)} %det_hbm.1, s32[4,4096]{1,0:T(4,128)} %pix_hbm.1, f32[64,128]{1,0:T(8,128)} %bitcast.5, f32[64,64]{1,0:T(8,128)} %mixing_hbm.1, f32[256,128]{1,0:T(8,128)} %bitcast.4), custom_call_target="tpu_custom_call" | custom-call | tf_op jit(solution)/shard_map/pallas_call | solution.py:497
  87.6 0.7 copy.11
  88.3 0.6 copy.12

commit v5 on v4

--- a/solution.py
+++ b/solution.py
@@ -54,7 +54,6 @@
     mixing_ref,
     current,
     ent_ref,
-    templ_h,
     code_h,
     det_h,
     seg_h,
@@ -99,6 +98,7 @@
     me = lax.axis_index("det")
     block = lax.axis_index("tile")
     chunks = SAMP_DEV // LANES
+    detectors = groups * DETECTORS_LOCAL
     xring = groups // ZRING
     my_x, my_z = lax.div(me, ZRING), lax.rem(me, ZRING)
 
@@ -156,34 +156,38 @@
 
     lax.fori_loop(0, groups, find_entry, 0)
 
-    det_h[...] = jnp.zeros_like(det_h)
-    code_h[...] = jnp.zeros_like(code_h)
-    clean_h[...] = jnp.zeros_like(clean_h)
-    stack[...] = jnp.zeros_like(stack)
-    templ_h[...] = jnp.zeros_like(templ_h)
+    def rows_of(j):
+        return slice(DETECTORS_LOCAL * j, DETECTORS_LOCAL * (j + 1))
+
     loads[1].wait()
     for j in range(chunks):
-        code_h[8 * j : 8 * j + DETECTORS_LOCAL, :] = pix_ref[:, LANES * j : LANES * (j + 1)]
+        code_h[rows_of(j), :] = pix_ref[:, LANES * j : LANES * (j + 1)]
 
     loads[2].wait()
-    home = (chunks, 8, LANES)
+    home = (chunks * DETECTORS_LOCAL // 8, 8, LANES)
+    flat = (chunks * DETECTORS_LOCAL, LANES)
+    sublane = lax.broadcasted_iota(jnp.int32, (8, LANES), 0)
     position = (
-        lax.broadcasted_iota(jnp.int32, home, 0) * LANES + lax.broadcasted_iota(jnp.int32, home, 2)
-    )
-    sublane = lax.broadcasted_iota(jnp.int32, (8, LANES), 0)
+        lax.broadcasted_iota(jnp.int32, home, 0) * (8 // DETECTORS_LOCAL)
+        + lax.div(lax.broadcasted_iota(jnp.int32, home, 1), DETECTORS_LOCAL)
+    ) * LANES + lax.broadcasted_iota(jnp.int32, home, 2)
     ends = [jnp.int32(0)] * DETECTORS_LOCAL
     seg = jnp.zeros(home, jnp.int32)
     for n in range(BASELINE_COUNT):
         end = jnp.zeros((8, LANES), jnp.int32)
         for l in range(DETECTORS_LOCAL):
             ends[l] = ends[l] + len_ref[l, 0, n]
-            end = jnp.where(sublane == l, ends[l], end)
+            end = jnp.where(lax.rem(sublane, DETECTORS_LOCAL) == l, ends[l], end)
         seg += (position >= end[None]).astype(jnp.int32)
-    seg_h[...] = seg.reshape(8 * chunks, LANES)
+    seg_h[...] = seg.reshape(flat)
+
+    def fold(tile):
+        turned = jnp.concatenate([tile[DETECTORS_LOCAL:], tile[:DETECTORS_LOCAL]], axis=0)
+        return tile + turned
 
     def entry_rows(e):
         l, k = entry_place(e)
-        return pl.ds(8 * HALF * k + l, HALF, stride=8)
+        return pl.ds(DETECTORS_LOCAL * HALF * k + l, HALF, stride=DETECTORS_LOCAL)
 
     for e in range(ENTRIES):
         code_e[e] = (
@@ -208,31 +212,28 @@
         copy_to(send_i.at[o], recv_i.at[me], sent.at[0], sem_i.at[me], det=o).start()
 
     for j in range(chunks):
-        det_h[8 * j : 8 * j + DETECTORS_LOCAL, :] = det_ref[:, LANES * j : LANES * (j + 1)]
+        det_h[rows_of(j), :] = det_ref[:, LANES * j : LANES * (j + 1)]
     table[...] = current[...].astype(jnp.bfloat16).astype(jnp.float32)
     templates = templ_ref[...].T
-    for d in range(groups):
-        templ_h[8 * d : 8 * d + DETECTORS_LOCAL, :] = templates[
-            DETECTORS_LOCAL * d : DETECTORS_LOCAL * (d + 1), :
-        ]
     mixed = jnp.dot(
-        templ_h[...], mixing_ref[...],
+        templates, mixing_ref[...],
         precision=lax.Precision.HIGHEST, preferred_element_type=jnp.float32,
     )
-    matrix[...] = lax.dot_general(
-        mixed, templ_h[...], (((1,), (1,)), ((), ())),
+    whole = jnp.dot(
+        mixed, templ_ref[...],
         precision=lax.Precision.HIGHEST, preferred_element_type=jnp.float32,
     )
+    high = whole.astype(jnp.bfloat16)
+    matrix[0:detectors, :] = high
+    matrix[detectors:, :] = (whole - high.astype(jnp.float32)).astype(jnp.bfloat16)
     def turn_columns():
         column = jnp.bitwise_and(recv_i[...].reshape(groups * HALF, LANES), COLS - 1).T
         for part in range(groups * HALF // LANES):
             columns[part] = column[:, LANES * part : LANES * (part + 1)]
 
-    def flags(part):
-        slots = LANES // HALF
-
+    def flags(part, first, last):
         def one(i, carry):
-            d = slots * part + i
+            d = LANES // HALF * part + i
             code = recv_i[d]
             row = jnp.where(
                 code < 0, -1, jnp.bitwise_and(lax.shift_right_arithmetic(code, 8), ROWS - 1)
@@ -253,21 +254,27 @@
                     ).astype(jnp.float32).astype(jnp.bfloat16)
             return carry
 
-        lax.fori_loop(0, slots, one, 0)
-
-    def peer_of(step):
-        x = lax.rem(my_x + lax.div(step, ZRING), xring)
-        z = lax.rem(my_z + lax.rem(step, ZRING), ZRING)
+        lax.fori_loop(first, last, one, 0)
+
+    def zigzag(i, size):
+        return size // 2 + lax.div(i + 1, 2) * (1 - 2 * lax.rem(i, 2))
+
+    def far_peer(step):
+        x = lax.rem(my_x + zigzag(lax.rem(step, xring), xring), xring)
+        z = lax.rem(my_z + zigzag(lax.div(step, xring), ZRING), ZRING)
         return x * ZRING + z
 
-    baseline = [jnp.zeros((8, 1), jnp.float32) for _ in range(BASELINE_COUNT)]
+    def near_peer(step):
+        return far_peer(groups - 1 - step)
+
+    baseline = jnp.zeros((8, LANES), jnp.float32)
 
     for it in range(ITERS):
         base_sem = 1 + 6 * it
 
         def answer(batch, carry):
             slots = [
-                peer_of(step if it == 0 else lax.rem(step + 20, groups))
+                near_peer(step) if it == 0 else far_peer(step)
                 for step in (TOGETHER * batch + i for i in range(TOGETHER))
             ]
             if it == 0:
@@ -309,42 +316,49 @@
         recv_a[it, me] = send_a[it, me]
         if it == 0:
             turn_columns()
-            flags(0)
+            flags(0, 0, 8)
         wait_bytes(recv_a.at[it], groups - 1, sem_a.at[it])
 
         for e in range(ENTRIES):
             work[entry_rows(e), :] = recv_a[it, owners[e]].astype(jnp.float32)
         residual = det_h[...] - work[...]
         for j in range(chunks):
-            send_b[it, j] = residual[8 * j : 8 * j + DETECTORS_LOCAL, :]
+            send_b[it, j] = residual[rows_of(j), :]
         recv_b[it, me] = send_b[it, me]
         for j in far:
             copy_to(
                 send_b.at[it, j], recv_b.at[it, me], sent.at[base_sem + 1], sem_b.at[it], det=j
             ).start()
         if it == 0:
-            flags(1)
+            flags(0, 8, 16)
+            flags(1, 0, 4)
         wait_bytes(recv_b.at[it], groups - 1, sem_b.at[it])
 
         for d in range(groups):
-            stack[8 * d : 8 * d + DETECTORS_LOCAL, :] = recv_b[it, d]
+            stack[rows_of(d), :] = recv_b[it, d]
         every = stack[...]
-        every = every - jnp.dot(
-            matrix[...], every,
-            precision=lax.Precision.HIGHEST, preferred_element_type=jnp.float32,
+        high = every.astype(jnp.bfloat16)
+        low = (every - high.astype(jnp.float32)).astype(jnp.bfloat16)
+        both = jnp.dot(matrix[...], high, preferred_element_type=jnp.float32)
+        every = every - (
+            both[0:detectors, :]
+            + both[detectors:, :]
+            + jnp.dot(matrix[0:detectors, :], low, preferred_element_type=jnp.float32)
         )
         for d in range(groups):
-            send_c[it, d] = every[8 * d : 8 * d + DETECTORS_LOCAL, :]
+            send_c[it, d] = every[rows_of(d), :]
         recv_c[it, me] = send_c[it, me]
         for d in far:
             copy_to(
                 send_c.at[it, d], recv_c.at[it, me], sent.at[base_sem + 2], sem_c.at[it], det=d
             ).start()
         acc[...] = jnp.zeros_like(acc)
+        if it == 0:
+            flags(1, 4, 16)
         wait_bytes(recv_c.at[it], groups - 1, sem_c.at[it])
 
         for j in range(chunks):
-            clean_h[8 * j : 8 * j + DETECTORS_LOCAL, :] = recv_c[it, j]
+            clean_h[rows_of(j), :] = recv_c[it, j]
         cleaned = clean_h[...].reshape(home)
         send_d[it] = jnp.sum(cleaned * cleaned, axis=0)
         recv_d[it, block] = send_d[it]
@@ -361,25 +375,30 @@
             ).start()
         recv_e[it, me] = val_e[jnp.maximum(ent_ref[me], 0)]
         wait_bytes(recv_d.at[it], blocks - 1, sem_d.at[it])
-        squares = jnp.sum(jnp.sum(recv_d[it], axis=0), axis=1, keepdims=True)
+        squares = fold(jnp.sum(recv_d[it], axis=0))
+        squares = jnp.sum(squares, axis=1, keepdims=True)
         level = HUBER * jnp.sqrt(squares / (SAMP_DEV * blocks) + EPS)
         weight = level[None] / jnp.maximum(jnp.abs(cleaned), level[None])
         weighted = weight * cleaned
         seg = seg_h[...].reshape(home)
         lane = lax.broadcasted_iota(jnp.int32, (8, LANES), 1)
-        line = jnp.where(lane == BASELINE_COUNT, level, 0.0)
-        increments = []
+        numerator = jnp.zeros((8, LANES), jnp.float32)
+        denominator = jnp.zeros((8, LANES), jnp.float32)
         for n in range(BASELINE_COUNT):
             inside = seg == n
-            numerator = jnp.sum(
-                jnp.sum(jnp.where(inside, weighted, 0.0), axis=0), axis=1, keepdims=True
+            numerator = jnp.where(
+                lane == n,
+                jnp.sum(jnp.sum(jnp.where(inside, weighted, 0.0), axis=0), axis=1, keepdims=True),
+                numerator,
             )
-            denominator = jnp.sum(
-                jnp.sum(jnp.where(inside, weight, 0.0), axis=0), axis=1, keepdims=True
+            denominator = jnp.where(
+                lane == n,
+                jnp.sum(jnp.sum(jnp.where(inside, weight, 0.0), axis=0), axis=1, keepdims=True),
+                denominator,
             )
-            increment = numerator / jnp.where(denominator > 0.0, denominator, 1.0)
-            increments.append(increment)
-            line = jnp.where(lane == n, increment, line)
+        denominator = fold(denominator)
+        increment = fold(numerator) / jnp.where(denominator > 0.0, denominator, 1.0)
+        line = jnp.where(lane == BASELINE_COUNT, level, increment)
         for l in range(DETECTORS_LOCAL):
             head[l] = line[l : l + 1, :]
         for o in near:
@@ -388,16 +407,15 @@
                 send_h.at[it, o], recv_h.at[it, me], sent.at[base_sem + 5], sem_h.at[it, me], det=o
             ).start()
         recv_h[it, me] = head[lax.div(jnp.maximum(ent_ref[me], 0), SEG_PER)]
-        for n in range(BASELINE_COUNT):
-            baseline[n] = baseline[n] + increments[n]
+        baseline = baseline + increment
         if it + 1 < ITERS:
             stepped = jnp.zeros(home, jnp.float32)
             for n in range(BASELINE_COUNT):
-                stepped = jnp.where(seg == n, increments[n][None], stepped)
-            det_h[...] = det_h[...] - stepped.reshape(8 * chunks, LANES)
+                stepped = jnp.where(seg == n, increment[:, n : n + 1][None], stepped)
+            det_h[...] = det_h[...] - stepped.reshape(flat)
 
         def collect(batch, carry):
-            slots = [peer_of(TOGETHER * batch + i) for i in range(TOGETHER)]
+            slots = [near_peer(TOGETHER * batch + i) for i in range(TOGETHER)]
             for i, d in enumerate(slots):
                 @pl.when(TOGETHER * batch + i > 0)
                 def _():
@@ -468,12 +486,8 @@
             table[...] = current[...].astype(jnp.bfloat16).astype(jnp.float32)
 
     sky_out[...] = current[...]
-    lane = lax.broadcasted_iota(jnp.int32, (8, LANES), 1)
-    fit = jnp.zeros((8, LANES), jnp.float32)
-    for n in range(BASELINE_COUNT):
-        fit = jnp.where(lane == n, baseline[n], fit)
     for l in range(DETECTORS_LOCAL):
-        base_out[l] = fit[l : l + 1, 0:BASELINE_COUNT]
+        base_out[l] = baseline[l : l + 1, 0:BASELINE_COUNT]
 
     wait_bytes(send_i, groups - 1, sent.at[0])
     for it in range(ITERS):
@@ -511,16 +525,15 @@
             pltpu.VMEM((MODES, MODES), f32),
             pltpu.VMEM((TILE_DEV * SIDE, SIDE), f32),
             pltpu.SMEM((groups,), i32),
-            pltpu.VMEM((8 * groups, MODES), f32),
-            pltpu.VMEM((8 * chunks, LANES), i32),
-            pltpu.VMEM((8 * chunks, LANES), f32),
-            pltpu.VMEM((8 * chunks, LANES), i32),
+            pltpu.VMEM((DETECTORS_LOCAL * chunks, LANES), i32),
+            pltpu.VMEM((DETECTORS_LOCAL * chunks, LANES), f32),
+            pltpu.VMEM((DETECTORS_LOCAL * chunks, LANES), i32),
             pltpu.VMEM((ENTRIES, HALF, LANES), i32),
             pltpu.VMEM((ENTRIES, HALF, LANES), f32),
-            pltpu.VMEM((8 * chunks, LANES), f32),
-            pltpu.VMEM((8 * chunks, LANES), f32),
-            pltpu.VMEM((8 * groups, LANES), f32),
-            pltpu.VMEM((8 * groups, 8 * groups), f32),
+            pltpu.VMEM((DETECTORS_LOCAL * chunks, LANES), f32),
+            pltpu.VMEM((DETECTORS_LOCAL * chunks, LANES), f32),
+            pltpu.VMEM((DETECTORS_LOCAL * groups, LANES), f32),
+            pltpu.VMEM((2 * DETECTORS_LOCAL * groups, DETECTORS_LOCAL * groups), bf16),
             pltpu.VMEM((TILE_DEV * SIDE, SIDE), f32),
             pltpu.VMEM((TOGETHER, SIDE, SIDE), f32),
             pltpu.VMEM((TOGETHER, TERMS, HALF, LANES), f32),

time: 89 us -> 85.7 us (0.963)
  Pallas kernels: 87 us -> 83.8 us
    pallas_call x1, Pallas kernels: 87 us -> 83.8 us  [local(): pl.pallas_call(functools.partial(kernel, groups, blocks), out_shape=(jax....]
where the time goes in v5:
time: 85.7 us
  Pallas kernels  83.8 us (98%)
  local copies, waits for them, and re-layouts  1.24 us (1%)
    pallas_call x1, Pallas kernels, local(): pl.pallas_call(functools.partial(kernel, groups, blocks), out_shape=(jax....  83.8 us

profile of v5, /device:TPU:1, one launch (start us, length us, event | category | flops | bytes accessed | tf_op | source)
XLA Modules:
  0.0 85.7 jit_solution(8315037114874659223)
XLA Ops:
  0.6 83.8 %shard_map.86 = (f32[256,128]{1,0:T(8,128)S(1)}, f32[4,1,16]{2,1,0:T(1,128)S(1)}) custom-call(s32[4,1,4]{2,1,0:T(1,128)} %cross_hbm.1, s32[4,1,16]{2,1,0:T(1,128)} %len_hbm.1, f32[4,4096]{1,0:T(4,128)} %det_hbm.1, s32[4,4096]{1,0:T(4,128)} %pix_hbm.1, f32[64,128]{1,0:T(8,128)} %bitcast.5, f32[64,64]{1,0:T(8,128)} %mixing_hbm.1, f32[256,128]{1,0:T(8,128)} %bitcast.4), custom_call_target="tpu_custom_call" | custom-call | tf_op jit(solution)/shard_map/pallas_call | solution.py:511
  84.4 0.7 copy.11
  85.1 0.6 copy.12

commit v6 on v5

--- a/solution.py
+++ b/solution.py
@@ -22,10 +22,9 @@
 COLS = 256
 ROWS = PIX // COLS
 HALF = PART // LANES
-TERMS = 3
-SEG_BITS = 16
-SEG_UNIT = 1 << SEG_BITS
+TERMS = 4
 TOGETHER = 4
+MANY = 8
 VMEM_BYTES = 32 * 1024 * 1024
 
 HUBER = 1.345
@@ -72,6 +71,10 @@
     rowoh,
     send_i,
     recv_i,
+    seg_e,
+    send_s,
+    recv_s,
+    code_g,
     send_a,
     recv_a,
     send_b,
@@ -88,6 +91,7 @@
     load_sem,
     sent,
     sem_i,
+    sem_s,
     sem_a,
     sem_b,
     sem_c,
@@ -193,13 +197,13 @@
         code_e[e] = (
             code_h[entry_rows(e), :]
             + lax.rem(tiles[e], TILE_DEV) * PIX
-            + seg_h[entry_rows(e), :] * SEG_UNIT
         )
+        seg_e[e] = seg_h[entry_rows(e), :].astype(jnp.int16)
 
     def pack_codes(o, carry):
         e = ent_ref[o]
         rows = code_e[jnp.maximum(e, 0)]
-        send_i[o] = jnp.where(jnp.full(rows.shape, e, jnp.int32) >= 0, rows, -1)
+        send_i[o] = jnp.where(jnp.full(rows.shape, e, jnp.int32) >= 0, rows, -1).astype(jnp.int16)
         return carry
 
     lax.fori_loop(0, groups, pack_codes, 0)
@@ -210,6 +214,11 @@
     pl.semaphore_wait(barrier, groups - 1 + blocks - 1)
     for o in near:
         copy_to(send_i.at[o], recv_i.at[me], sent.at[0], sem_i.at[me], det=o).start()
+
+    for o in near:
+        send_s[o] = seg_e[jnp.maximum(ent_ref[o], 0)]
+        copy_to(send_s.at[o], recv_s.at[me], sent.at[1], sem_s, det=o).start()
+    recv_s[me] = seg_e[jnp.maximum(ent_ref[me], 0)]
 
     for j in range(chunks):
         det_h[rows_of(j), :] = det_ref[:, LANES * j : LANES * (j + 1)]
@@ -227,14 +236,14 @@
     matrix[0:detectors, :] = high
     matrix[detectors:, :] = (whole - high.astype(jnp.float32)).astype(jnp.bfloat16)
     def turn_columns():
-        column = jnp.bitwise_and(recv_i[...].reshape(groups * HALF, LANES), COLS - 1).T
+        column = jnp.bitwise_and(code_g[...].reshape(groups * HALF, LANES), COLS - 1).T
         for part in range(groups * HALF // LANES):
             columns[part] = column[:, LANES * part : LANES * (part + 1)]
 
     def flags(part, first, last):
         def one(i, carry):
             d = LANES // HALF * part + i
-            code = recv_i[d]
+            code = code_g[d]
             row = jnp.where(
                 code < 0, -1, jnp.bitwise_and(lax.shift_right_arithmetic(code, 8), ROWS - 1)
             )
@@ -270,7 +279,7 @@
     baseline = jnp.zeros((8, LANES), jnp.float32)
 
     for it in range(ITERS):
-        base_sem = 1 + 6 * it
+        base_sem = 2 + 6 * it
 
         def answer(batch, carry):
             slots = [
@@ -286,7 +295,9 @@
                         ).wait_recv()
             values = []
             for i, d in enumerate(slots):
-                code = recv_i[d]
+                if it == 0:
+                    code_g[d] = recv_i[d].astype(jnp.int32)
+                code = code_g[d]
                 row = jnp.bitwise_and(lax.shift_right_arithmetic(code, 7), SIDE - 1)
                 col = jnp.bitwise_and(code, LANES - 1)
                 second = jnp.bitwise_and(code, PIX) > 0
@@ -414,10 +425,13 @@
                 stepped = jnp.where(seg == n, increment[:, n : n + 1][None], stepped)
             det_h[...] = det_h[...] - stepped.reshape(flat)
 
-        def collect(batch, carry):
-            slots = [near_peer(TOGETHER * batch + i) for i in range(TOGETHER)]
+        if it == 0:
+            wait_bytes(recv_s, groups - 1, sem_s)
+
+        def collect(first, count):
+            slots = [near_peer(first + i) for i in range(count)]
             for i, d in enumerate(slots):
-                @pl.when(TOGETHER * batch + i > 0)
+                @pl.when(d != me)
                 def _():
                     copy_to(
                         send_e.at[it, d], recv_e.at[it, d], sent.at[base_sem + 4], sem_e.at[it, d],
@@ -430,9 +444,7 @@
             for i, d in enumerate(slots):
                 cleaned_d = recv_e[it, d]
                 line = jnp.broadcast_to(recv_h[it, d], (HALF, LANES))
-                seg_d = jnp.bitwise_and(
-                    lax.shift_right_arithmetic(recv_i[d], SEG_BITS), BASELINE_COUNT - 1
-                )
+                seg_d = recv_s[d].astype(jnp.int32)
                 step_d = jnp.take_along_axis(line, seg_d, axis=1)
                 level_d = jnp.take_along_axis(
                     line, jnp.full((HALF, LANES), BASELINE_COUNT, jnp.int32), axis=1
@@ -442,7 +454,9 @@
                 high = value_d.astype(jnp.bfloat16).astype(jnp.float32)
                 parts[i, 0] = high
                 parts[i, 1] = value_d - high
-                parts[i, 2] = weight_d
+                high = weight_d.astype(jnp.bfloat16).astype(jnp.float32)
+                parts[i, 2] = high
+                parts[i, 3] = weight_d - high
             sums = []
             for i, d in enumerate(slots):
                 weighed = jnp.concatenate(
@@ -464,7 +478,7 @@
                 spread = jnp.concatenate([coloh[d, h] for h in range(COLS // LANES)], axis=1)
                 product = jnp.dot(weighed, spread, preferred_element_type=jnp.float32)
                 second = (
-                    jnp.broadcast_to(jnp.bitwise_and(recv_i[d], PIX)[0:1, 0:1], product.shape) > 0
+                    jnp.broadcast_to(jnp.bitwise_and(code_g[d], PIX)[0:1, 0:1], product.shape) > 0
                 )
                 sums.append((jnp.where(second, 0.0, product), jnp.where(second, product, 0.0)))
             for t in range(TILE_DEV):
@@ -472,12 +486,20 @@
                 for part in sums[1:]:
                     total = total + part[t]
                 acc[t] += total
+
+        def collect_many(batch, carry):
+            collect(TOGETHER + MANY * batch, MANY)
             return carry
 
-        lax.fori_loop(0, groups // TOGETHER, collect, 0)
+        collect(0, TOGETHER)
+        many = (groups - TOGETHER) // MANY
+        lax.fori_loop(0, many, collect_many, 0)
+        rest = TOGETHER + MANY * many
+        if rest < groups:
+            collect(rest, groups - rest)
         for t in range(TILE_DEV):
             change = (acc[t, 0:ROWS, :] + acc[t, ROWS : 2 * ROWS, :]) / jnp.maximum(
-                acc[t, 2 * ROWS : 3 * ROWS, :], 1.0
+                acc[t, 2 * ROWS : 3 * ROWS, :] + acc[t, 3 * ROWS : 4 * ROWS, :], 1.0
             )
             for half in range(2):
                 rows = pl.ds(SIDE * t + half, ROWS, stride=2)
@@ -490,8 +512,9 @@
         base_out[l] = baseline[l : l + 1, 0:BASELINE_COUNT]
 
     wait_bytes(send_i, groups - 1, sent.at[0])
+    wait_bytes(send_s, groups - 1, sent.at[1])
     for it in range(ITERS):
-        base_sem = 1 + 6 * it
+        base_sem = 2 + 6 * it
         wait_bytes(send_a.at[it], groups - 1, sent.at[base_sem])
         wait_bytes(send_b.at[it], groups - 1, sent.at[base_sem + 1])
         wait_bytes(send_c.at[it], groups - 1, sent.at[base_sem + 2])
@@ -506,7 +529,7 @@
     chunks = SAMP_DEV // LANES
     vmem = pl.BlockSpec(memory_space=pltpu.VMEM)
     hbm = pl.BlockSpec(memory_space=pltpu.HBM)
-    f32, bf16, i32 = jnp.float32, jnp.bfloat16, jnp.int32
+    f32, bf16, i32, i16 = jnp.float32, jnp.bfloat16, jnp.int32, jnp.int16
     dma = pltpu.SemaphoreType.DMA
     sky, fit = pl.pallas_call(
         functools.partial(kernel, groups, blocks),
@@ -536,12 +559,16 @@
             pltpu.VMEM((2 * DETECTORS_LOCAL * groups, DETECTORS_LOCAL * groups), bf16),
             pltpu.VMEM((TILE_DEV * SIDE, SIDE), f32),
             pltpu.VMEM((TOGETHER, SIDE, SIDE), f32),
-            pltpu.VMEM((TOGETHER, TERMS, HALF, LANES), f32),
+            pltpu.VMEM((MANY, TERMS, HALF, LANES), f32),
             pltpu.VMEM((TILE_DEV, TERMS * ROWS, COLS), f32),
             pltpu.VMEM((groups * HALF // LANES, LANES, LANES), i32),
             pltpu.VMEM((groups, COLS // LANES, PART, LANES), bf16),
             pltpu.VMEM((groups, HALF, ROWS, LANES), bf16),
-            pltpu.VMEM((groups, HALF, LANES), i32),
+            pltpu.VMEM((groups, HALF, LANES), i16),
+            pltpu.VMEM((groups, HALF, LANES), i16),
+            pltpu.VMEM((ENTRIES, HALF, LANES), i16),
+            pltpu.VMEM((groups, HALF, LANES), i16),
+            pltpu.VMEM((groups, HALF, LANES), i16),
             pltpu.VMEM((groups, HALF, LANES), i32),
             pltpu.VMEM((ITERS, groups, HALF, LANES), bf16),
             pltpu.VMEM((ITERS, groups, HALF, LANES), bf16),
@@ -557,8 +584,9 @@
             pltpu.VMEM((ITERS, groups, 1, LANES), f32),
             pltpu.VMEM((ITERS, groups, 1, LANES), f32),
             dma((7,)),
-            dma((1 + 6 * ITERS,)),
+            dma((2 + 6 * ITERS,)),
             dma((groups,)),
+            dma,
             dma((ITERS,)),
             dma((ITERS,)),
             dma((ITERS,)),

time: 85.7 us -> 86.2 us (level)
  no operation moved by 1% of the time
where the time goes in v6:
time: 86.2 us; the launch traced here: 86.1 us
  Pallas kernels  84.2 us (98%)
  local copies, waits for them, and re-layouts  1.24 us (1%)
    pallas_call x1, Pallas kernels, local(): pl.pallas_call(functools.partial(kernel, groups, blocks), out_shape=(jax....  84.2 us

profile of v6, /device:TPU:1, one launch (start us, length us, event | category | flops | bytes accessed | tf_op | source)
XLA Modules:
  0.0 86.1 jit_solution(13041114047640521059)
XLA Ops:
  0.6 84.2 %shard_map.86 = (f32[256,128]{1,0:T(8,128)S(1)}, f32[4,1,16]{2,1,0:T(1,128)S(1)}) custom-call(s32[4,1,4]{2,1,0:T(1,128)} %cross_hbm.1, s32[4,1,16]{2,1,0:T(1,128)} %len_hbm.1, f32[4,4096]{1,0:T(4,128)} %det_hbm.1, s32[4,4096]{1,0:T(4,128)} %pix_hbm.1, f32[64,128]{1,0:T(8,128)} %bitcast.5, f32[64,64]{1,0:T(8,128)} %mixing_hbm.1, f32[256,128]{1,0:T(8,128)} %bitcast.4), custom_call_target="tpu_custom_call" | custom-call | tf_op jit(solution)/shard_map/pallas_call | solution.py:534
  84.8 0.7 copy.11
  85.5 0.6 copy.12

commit v7 on v6

--- a/solution.py
+++ b/solution.py
@@ -477,6 +477,14 @@
                 )
                 spread = jnp.concatenate([coloh[d, h] for h in range(COLS // LANES)], axis=1)
                 product = jnp.dot(weighed, spread, preferred_element_type=jnp.float32)
+                product = jnp.concatenate(
+                    [
+                        product[2 * t * ROWS : (2 * t + 1) * ROWS, :]
+                        + product[(2 * t + 1) * ROWS : (2 * t + 2) * ROWS, :]
+                        for t in range(TERMS // 2)
+                    ],
+                    axis=0,
+                )
                 second = (
                     jnp.broadcast_to(jnp.bitwise_and(code_g[d], PIX)[0:1, 0:1], product.shape) > 0
                 )
@@ -498,9 +506,7 @@
         if rest < groups:
             collect(rest, groups - rest)
         for t in range(TILE_DEV):
-            change = (acc[t, 0:ROWS, :] + acc[t, ROWS : 2 * ROWS, :]) / jnp.maximum(
-                acc[t, 2 * ROWS : 3 * ROWS, :] + acc[t, 3 * ROWS : 4 * ROWS, :], 1.0
-            )
+            change = acc[t, 0:ROWS, :] / jnp.maximum(acc[t, ROWS : 2 * ROWS, :], 1.0)
             for half in range(2):
                 rows = pl.ds(SIDE * t + half, ROWS, stride=2)
                 current[rows, :] = current[rows, :] + change[:, LANES * half : LANES * (half + 1)]
@@ -560,7 +566,7 @@
             pltpu.VMEM((TILE_DEV * SIDE, SIDE), f32),
             pltpu.VMEM((TOGETHER, SIDE, SIDE), f32),
             pltpu.VMEM((MANY, TERMS, HALF, LANES), f32),
-            pltpu.VMEM((TILE_DEV, TERMS * ROWS, COLS), f32),
+            pltpu.VMEM((TILE_DEV, TERMS // 2 * ROWS, COLS), f32),
             pltpu.VMEM((groups * HALF // LANES, LANES, LANES), i32),
             pltpu.VMEM((groups, COLS // LANES, PART, LANES), bf16),
             pltpu.VMEM((groups, HALF, ROWS, LANES), bf16),

time: 86.2 us -> 86 us (level)
  no operation moved by 1% of the time
where the time goes in v7:
time: 86 us; the launch traced here: 85.9 us
  Pallas kernels  84 us (98%)
  local copies, waits for them, and re-layouts  1.24 us (1%)
    pallas_call x1, Pallas kernels, local(): pl.pallas_call(functools.partial(kernel, groups, blocks), out_shape=(jax....  84 us

profile of v7, /device:TPU:1, one launch (start us, length us, event | category | flops | bytes accessed | tf_op | source)
XLA Modules:
  0.0 85.9 jit_solution(11383474036892576620)
XLA Ops:
  0.6 84.0 %shard_map.86 = (f32[256,128]{1,0:T(8,128)S(1)}, f32[4,1,16]{2,1,0:T(1,128)S(1)}) custom-call(s32[4,1,4]{2,1,0:T(1,128)} %cross_hbm.1, s32[4,1,16]{2,1,0:T(1,128)} %len_hbm.1, f32[4,4096]{1,0:T(4,128)} %det_hbm.1, s32[4,4096]{1,0:T(4,128)} %pix_hbm.1, f32[64,128]{1,0:T(8,128)} %bitcast.5, f32[64,64]{1,0:T(8,128)} %mixing_hbm.1, f32[256,128]{1,0:T(8,128)} %bitcast.4), custom_call_target="tpu_custom_call" | custom-call | tf_op jit(solution)/shard_map/pallas_call | solution.py:540
  84.6 0.7 copy.11
  85.3 0.6 copy.12
